TPU v7x, 32 devices: a whole 2x2x4 slice. The times are simulated.
32 devices in a mesh: row: 4 (over z), col: 8 (over y, x, core).
Axes of the slice: x: 2, y: 2, z: 4, core: 2. Of those that a mesh axis runs over, the one named last changes fastest.
Arguments:
- inverse_top: bfloat16 [1024, 1024], P('col', 'row'), may hold values from -0.1875 to 0.1875
- inverse_one: bfloat16 [1536, 768], P('col', 'row'), may hold values from -0.21875 to 0.21875
- inverse_two: bfloat16 [2048, 512], P('col', 'row'), may hold values from -0.25 to 0.25
- inverse_leaf: bfloat16 [2048, 256], P('col', 'row'), may hold values from -0.375 to 0.375
- coupling_one: bfloat16 [768, 1536], P('row', 'col'), may hold values from -0.21875 to 0.21875
- coupling_two: bfloat16 [512, 2048], P('row', 'col'), may hold values from -0.25 to 0.25
- coupling_leaf: bfloat16 [256, 2048], P('row', 'col'), may hold values from -0.375 to 0.375
- rhs_top: bfloat16 [1024, 256], P('row', 'col'), may hold values from -6 to 6
- rhs_one: bfloat16 [768, 512], P('row', 'col'), may hold values from -6 to 6
- rhs_two: bfloat16 [512, 1024], P('row', 'col'), may hold values from -6 to 6
- rhs_leaf: bfloat16 [256, 2048], P('row', 'col'), may hold values from -6 to 6
- parent_map_one: int32 [2, 768], replicated, may hold values from 0 to 1023, as said below
- parent_map_two: int32 [4, 512], replicated, may hold values from 0 to 1535, as said below
- parent_map_leaf: int32 [8, 256], replicated, may hold values from 0 to 1023, as said below
Outputs:
- solution_top: bfloat16 [1024, 256], P('row', 'col')
- solution_one: bfloat16 [768, 512], P('row', 'col')
- solution_two: bfloat16 [512, 1024], P('row', 'col')
- solution_leaf: bfloat16 [256, 2048], P('row', 'col')
Inputs may be any that keep to these rules, and one draw needn't show every extreme that they name: `parent_map_one`: row k lists distinct rows of the top front, one for each of the 768 update rows of front k. Cut the update rows and the top separator each into 4 equal blocks: at most 96 rows of one block land in one block of the top front, a number that is reached in every row, and every block of the top front receives exactly 192 rows from each child. `parent_map_two`: row k lists distinct rows of the front k // 2 of the second level (its 768 separator rows first, then its 768 update rows), one for each of the 512 update rows of front k. Cut the update rows into 4 equal blocks, and the parent's separator rows and its update rows each into 4 equal blocks, block j of the parent being the j-th separator block with the j-th update block: at most 64 rows of one block land in one parent block, reached in every row, and every parent block receives exactly 128 rows from each child. `parent_map_leaf`: as for parent_map_two, one level lower: 256 update rows of front k into front k // 2 of the third level, at most 32 rows of one block into one parent block, reached in every row, and exactly 64 rows from each child into every parent block.
All inputs are finite; a program needn't handle non-finite values.
Results may differ from a plain program's by a relative error of at most 0.03.
Values may be sent and summed in bfloat16 or wider, within the bound.
A program may use at most 64 MiB of HBM per device.

v0:
```python
import jax
import jax.numpy as jnp
from jax import lax
from jax.experimental import pallas as pl
from jax.experimental.pallas import tpu as pltpu
from jax.sharding import PartitionSpec as P


def swapped(value, axis, stride):
    mask = 2**stride
    pairs = [(source, source ^ mask) for source in range(lax.axis_size(axis))]
    return lax.ppermute(value, axis, pairs)


def route_tables(mapping, child_index, parent_sep, parent_upd, strips, row_index):
    positions = lax.dynamic_index_in_dim(mapping, child_index, 0, keepdims=False)
    sep_rows = parent_sep // strips
    in_separator = positions < parent_sep
    if parent_upd > 0:
        upd_rows = parent_upd // strips
        target = jnp.where(
            in_separator, positions // sep_rows, (positions - parent_sep) // upd_rows
        )
        offset = jnp.where(
            in_separator, positions % sep_rows, sep_rows + (positions - parent_sep) % upd_rows
        )
    else:
        target = positions // sep_rows
        offset = positions % sep_rows
    block_rows = positions.shape[0] // strips
    blocks = target.reshape(strips, block_rows)
    matches = (blocks[:, :, None] == jnp.arange(strips, dtype=jnp.int32)[None, None, :]).astype(
        jnp.int32
    )
    slot_of = jnp.sum((jnp.cumsum(matches, axis=1) - 1) * matches, axis=2).reshape(-1)
    block_len = sep_rows + parent_upd // strips
    capacity = 2 * positions.shape[0] // (strips * strips)
    source = jnp.arange(positions.shape[0], dtype=jnp.int32) // block_rows
    mine_here = target == row_index
    column_at = jnp.where(mine_here, slot_of, capacity)
    lookup = jnp.full((strips, capacity + 1), block_len, jnp.int32)
    lookup = lookup.at[source, column_at].set(jnp.where(mine_here, offset, block_len))[:, :capacity]
    local_target = lax.dynamic_slice_in_dim(target, row_index * block_rows, block_rows)
    local_slots = lax.dynamic_slice_in_dim(slot_of, row_index * block_rows, block_rows)
    return (local_target, local_slots, lookup, capacity, block_len)


def pack_rows(values, local_target, local_slots, strips, capacity):
    buffer = jnp.zeros((strips, capacity, values.shape[1]), values.dtype)
    return buffer.at[local_target, local_slots].set(values)


def unpack_rows(received, lookup, block_len):
    summed = jnp.zeros((block_len + 1, received.shape[2]), jnp.float32)
    return summed.at[lookup].add(received.astype(jnp.float32))[:block_len]


def spread(portion, depth_bits, pass_on, column):
    for bit_index in range(depth_bits):
        partner = pass_on(portion, bit_index)
        is_upper = column >> bit_index & 1 == 1
        portion = jnp.where(
            is_upper,
            jnp.concatenate([partner, portion], axis=-1),
            jnp.concatenate([portion, partner], axis=-1),
        )
    return portion


def shrink(entire, depth_bits, pass_on, column):
    for bit_index in reversed(range(depth_bits)):
        half_width = entire.shape[-1] // 2
        low_part = entire[..., :half_width]
        high_part = entire[..., half_width:]
        is_upper = column >> bit_index & 1 == 1
        kept_part = jnp.where(is_upper, high_part, low_part)
        sent_part = jnp.where(is_upper, low_part, high_part)
        entire = kept_part + pass_on(sent_part, bit_index)
    return entire


def per_device(
    inverse_top,
    inverse_one,
    inverse_two,
    inverse_leaf,
    coupling_one,
    coupling_two,
    coupling_leaf,
    rhs_top,
    rhs_one,
    rhs_two,
    rhs_leaf,
    parent_map_one,
    parent_map_two,
    parent_map_leaf,
):
    strips = lax.axis_size("row")
    col_count = lax.axis_size("col")
    row_here = lax.axis_index("row")
    column = lax.axis_index("col")
    inverses = [inverse_top, inverse_one, inverse_two, inverse_leaf]
    couplings = [None, coupling_one, coupling_two, coupling_leaf]
    right_sides = [rhs_top, rhs_one, rhs_two, rhs_leaf]
    parent_maps = [None, parent_map_one, parent_map_two, parent_map_leaf]
    orders = [inverse.shape[1] * strips for inverse in inverses]
    groups = [col_count >> tree_level for tree_level in range(4)]
    group_bits = [group_size.bit_length() - 1 for group_size in groups]
    pass_rhs = lambda values, bit_index: swapped(values, "col", bit_index)
    pass_update_sum = lambda values, bit_index: swapped(
        values.astype(jnp.bfloat16), "col", bit_index
    ).astype(values.dtype)
    pass_update_spread = lambda values, bit_index: swapped(values, "col", bit_index)
    pass_solution_sum = lambda values, bit_index: swapped(
        values.astype(jnp.bfloat16), "col", bit_index
    ).astype(values.dtype)
    pass_solution_spread = lambda values, bit_index: swapped(values, "col", bit_index)
    full_rhs = [
        spread(right_sides[tree_level], group_bits[tree_level], pass_rhs, column)
        for tree_level in range(4)
    ]
    own_routes = [None]
    for tree_level in range(1, 4):
        parent_order = orders[tree_level - 1]
        parent_update = parent_order if tree_level > 1 else 0
        front_here = column // groups[tree_level]
        own_routes.append(
            route_tables(
                parent_maps[tree_level], front_here, parent_order, parent_update, strips, row_here
            )
        )
    pivots = [None] * 4
    incoming = None
    for tree_level in (3, 2, 1, 0):
        sep_rows = inverses[tree_level].shape[1]
        if incoming is None:
            separator = full_rhs[tree_level]
            own_update = None
        else:
            separator = (full_rhs[tree_level].astype(jnp.float32) + incoming[:sep_rows]).astype(
                jnp.bfloat16
            )
            own_update = lax.optimization_barrier(incoming[sep_rows:].astype(jnp.bfloat16))
        partial_value = jnp.dot(inverses[tree_level], separator, preferred_element_type=jnp.float32)
        solved = lax.psum(partial_value.astype(jnp.bfloat16), "row")
        pivots[tree_level] = solved
        if tree_level > 0:
            coupled = jnp.dot(couplings[tree_level], solved, preferred_element_type=jnp.float32)
            reduced = shrink(coupled, group_bits[tree_level], pass_update_sum, column)
            if own_update is None:
                portion = (-reduced).astype(jnp.bfloat16)
            else:
                start_at = column % groups[tree_level] * reduced.shape[1]
                kept_rows = lax.dynamic_slice_in_dim(own_update, start_at, reduced.shape[1], 1)
                portion = (kept_rows.astype(jnp.float32) - reduced).astype(jnp.bfloat16)
            updated = spread(portion, group_bits[tree_level], pass_update_spread, column)
            own_target, own_slots, own_lookup, capacity, block_len = own_routes[tree_level]
            got_own = lax.all_to_all(
                pack_rows(updated, own_target, own_slots, strips, capacity),
                "row",
                split_axis=0,
                concat_axis=0,
                tiled=True,
            )
            own_part = unpack_rows(got_own, own_lookup, block_len)
            partner = swapped(own_part.astype(jnp.bfloat16), "col", group_bits[tree_level])
            incoming = own_part + partner.astype(jnp.float32)
    solutions = [None] * 4
    parent_solution = None
    parent_gathered = None
    for tree_level in range(4):
        solved = pivots[tree_level]
        gathered = None
        if tree_level == 0:
            residual = solved
        else:
            own_target, own_slots, own_lookup, capacity, block_len = own_routes[tree_level]
            pieces = [parent_solution]
            if parent_gathered is not None:
                pieces.append(parent_gathered)
            pieces.append(jnp.zeros((1, parent_solution.shape[1]), jnp.bfloat16))
            parent_rows = jnp.concatenate(pieces, axis=0)
            returned = lax.all_to_all(
                parent_rows[own_lookup], "row", split_axis=0, concat_axis=0, tiled=True
            )
            gathered = returned[own_target, own_slots]
            coupling_term = jnp.dot(
                couplings[tree_level].T, gathered, preferred_element_type=jnp.float32
            )
            residual = (
                solved.astype(jnp.float32)
                - lax.psum(coupling_term.astype(jnp.bfloat16), "row").astype(jnp.float32)
            ).astype(jnp.bfloat16)
        contribution = jnp.dot(inverses[tree_level].T, residual, preferred_element_type=jnp.float32)
        if tree_level == 0:
            summed = lax.psum(contribution.astype(jnp.bfloat16), "col")
            solution = summed
            rhs_width = solution.shape[1] // groups[0]
            solutions[0] = lax.dynamic_slice_in_dim(
                solution, column % groups[0] * rhs_width, rhs_width, 1
            )
        else:
            portion = shrink(
                contribution, group_bits[tree_level], pass_solution_sum, column
            ).astype(jnp.bfloat16)
            solutions[tree_level] = portion
            if tree_level < 3:
                solution = spread(portion, group_bits[tree_level], pass_solution_spread, column)
        parent_solution = solution
        parent_gathered = gathered
    return (solutions[0], solutions[1], solutions[2], solutions[3])


MESH = pl.DeviceIdType.MESH


def dot_nn(left, right):
    return lax.dot_general(left, right, (((1,), (0,)), ((), ())), preferred_element_type=jnp.float32)


def dot_nt(left, right):
    return lax.dot_general(left, right, (((1,), (1,)), ((), ())), preferred_element_type=jnp.float32)


def eye(size):
    rows = lax.broadcasted_iota(jnp.int32, (size, size), 0)
    columns = lax.broadcasted_iota(jnp.int32, (size, size), 1)
    return jnp.where(rows == columns, 1.0, 0.0).astype(jnp.bfloat16)


def flipped(value, mask):
    result = value
    bit = 1
    while bit <= mask:
        if mask & bit:
            result = result + bit * (1 - 2 * ((value // bit) % 2))
        bit *= 2
    return result


class Plan:
    def __init__(self, rows, cols, inverse_shapes, rhs_top_shape):
        self.rows, self.cols = rows, cols
        self.strip = [shape[1] for shape in inverse_shapes]
        self.order = [shape[1] * rows for shape in inverse_shapes]
        self.local = [shape[0] for shape in inverse_shapes]
        self.group = [cols >> level for level in range(4)]
        self.columns = rhs_top_shape[1] * cols
        self.width = [self.columns // group if group else 0 for group in self.group]
        self.mine = self.columns // rows

    def total(self, level):
        return self.order[level] * (2 if level else 1)

    def fits(self):
        table = sum(
            2 * self.total(level) * self.order[level + 1] * 2 for level in range(3)
        )
        if self.rows < 3 or self.group[3] != 1 or self.mine * self.rows != self.columns or table > 24 * 2**20:
            return False
        for level in range(4):
            if self.strip[level] % 16 or self.order[level] % 128 or self.width[level] % 16:
                return False
            if max(self.width[level], self.mine) % min(self.width[level], self.mine):
                return False
        for level in (1, 2):
            if self.mine % (16 * self.group[level]):
                return False
        return self.order[0] % (128 * self.group[0]) == 0 and self.group[0] % self.rows == 0


def narrow(size):
    return size < 128


def build_kernel(plan):
    R, CC, N = plan.rows, plan.cols, plan.mine
    S, K, L, G, W = plan.order, plan.strip, plan.local, plan.group, plan.width
    bf = jnp.bfloat16
    scratch, names = [], {}

    def ref(name, shape, dtype=bf):
        names[name] = len(scratch)
        scratch.append(pltpu.VMEM(shape, dtype))

    def sems(name, shape):
        names[name] = len(scratch)
        scratch.append(pltpu.SemaphoreType.DMA(shape))

    for l in range(4):
        n_dest = max(1, W[l] // N)
        n_part = max(1, N // W[l])
        ref(f"Z{l}", (R, K[l], L[l]) if narrow(K[l]) else (R, L[l], K[l]))
        sems(f"Zs{l}", (2, R))
        sems(f"Zr{l}", (2, R))
        if l:
            ref(f"C{l}", (S[l], L[l]))
            sems(f"Cs{l}", (2, R))
            sems(f"Cr{l}", (2, R))
        ref(f"bT{l}", (W[l], K[l]))
        ref(f"B{l}", (R, N, K[l]))
        sems(f"Bs{l}", (n_dest,))
        sems(f"Br{l}", (R,))
        sems(f"Ds{l}", (G[l],))
        sems(f"Dr{l}", (n_part,))
        ref(f"y{l}", (N, L[l]))
        ref(f"fx{l}", (R, N, K[l]))
        ref(f"oT{l}", (W[l], K[l]))
        sems(f"Os{l}", (R,))
        sems(f"Or{l}", (n_dest,))
        if l < 3:
            ref(f"hot{l}", (2, plan.total(l), S[l + 1]))
            if l:
                shape = (G[l], R, N // G[l], K[l])
                ref(f"xp{l}", shape)
                ref(f"xr{l}", shape)
                ref(f"xs{l}", shape)
            else:
                shape = (G[0], N, S[0] // G[0])
                ref("xp0", shape)
                ref("xr0", shape)
                ref("xs0", shape)
            for tag in ("xps", "xpr", "xss", "xsr"):
                sems(f"{tag}{l}", (G[l],))
        if l:
            shape = (G[l], N // G[l], S[l])
            ref(f"u{l}", (2,) + shape)
            sems(f"us{l}", (2 * G[l],))
            sems(f"ur{l}", (2 * G[l],))
            ref(f"v{l}", (N, S[l]))
            if G[l] > 1:
                ref(f"H{l}", shape)
                ref(f"up{l}", shape)
                ref(f"ut{l}", shape)
                sems(f"ups{l}", (G[l],))
                sems(f"upr{l}", (G[l],))

    def kernel(*refs):
        inverse = refs[0:4]
        coupling = (None,) + tuple(refs[4:7])
        rhs = refs[7:11]
        maps = (None,) + tuple(refs[11:14])
        outs = refs[14:18]
        held = refs[18:]
        at = lambda name: held[names[name]]
        z = lax.axis_index("row")
        c = lax.axis_index("col")
        sent = []

        def remote(src, dst, ssem, rsem, z_to, c_to):
            return pltpu.make_async_remote_copy(
                src_ref=src, dst_ref=dst, send_sem=ssem, recv_sem=rsem,
                device_id=(z_to, c_to), device_id_type=MESH,
            )

        def send(src, dst, ssem, rsem, z_to, c_to):
            copy = remote(src, dst, ssem, rsem, z_to, c_to)
            copy.start()
            sent.append(copy.wait_send)

        def send_or_copy(src, dst, ssem, rsem, z_to, c_to, here):
            @pl.when(here)
            def _():
                pltpu.make_async_copy(src, dst, rsem).start()

            @pl.when(jnp.logical_not(here))
            def _():
                remote(src, dst, ssem, rsem, z_to, c_to).start()

            def finish():
                @pl.when(jnp.logical_not(here))
                def _():
                    remote(src, dst, ssem, rsem, z_to, c_to).wait_send()

            sent.append(finish)

        def arrived(dst, rsem):
            pltpu.make_async_copy(dst, dst, rsem).wait()

        barrier = pltpu.get_barrier_semaphore()
        for d in range(1, R):
            pl.semaphore_signal(
                barrier, inc=1, device_id=((z + d) % R, c), device_id_type=MESH
            )
        for m in range(1, CC):
            pl.semaphore_signal(
                barrier, inc=1, device_id=(z, flipped(c, m)), device_id_type=MESH
            )
        turned = []
        for l in range(4):
            if narrow(W[l]):
                turned.append(rhs[l])
            else:
                at(f"bT{l}")[...] = dot_nt(eye(W[l]), rhs[l][...]).astype(bf)
                turned.append(at(f"bT{l}"))
        pl.semaphore_wait(barrier, R + CC - 2)

        def start_rhs(l):
            q = c % G[l]
            n_dest, n_part = max(1, W[l] // N), max(1, N // W[l])
            for i in range(n_dest):
                if W[l] >= N:
                    z_to = q * n_dest + i
                    src = turned[l].at[pl.ds(i * N, N)]
                    dst = at(f"B{l}").at[z]
                else:
                    z_to = q // n_part
                    src = turned[l]
                    low = pl.multiple_of((q % n_part) * W[l], W[l])
                    dst = at(f"B{l}").at[z, pl.ds(low, W[l])]
                ssem, rsem = at(f"Bs{l}").at[i], at(f"Br{l}").at[z]
                send_or_copy(src, dst, ssem, rsem, z_to, c, z_to == z)

        def rhs_part(l, part):
            if W[l] >= N:
                return at(f"B{l}")
            return at(f"B{l}").at[:, pl.ds(pl.multiple_of(part * W[l], W[l]), W[l])]

        def spread_rhs(l):
            q = c % G[l]
            n_dest, n_part = max(1, W[l] // N), max(1, N // W[l])
            holds = z // n_dest == q // n_part
            part = q % n_part
            here = rhs_part(l, part)

            def copy_to(m):
                return remote(
                    here, here, at(f"Ds{l}").at[m], at(f"Dr{l}").at[part], z, flipped(c, m)
                )

            @pl.when(holds)
            def _():
                for r in range(R):
                    block = at(f"B{l}").at[r]
                    if n_part > 1:
                        low = pl.multiple_of(part * W[l], W[l])
                        block = at(f"B{l}").at[r, pl.ds(low, W[l])]
                    arrived(block, at(f"Br{l}").at[r])
                for m in range(1, G[l]):
                    copy_to(m).start()

            def finish():
                @pl.when(holds)
                def _():
                    for m in range(1, G[l]):
                        copy_to(m).wait_send()

            sent.append(finish)

        def wait_rhs(l):
            q = c % G[l]
            n_dest, n_part = max(1, W[l] // N), max(1, N // W[l])
            for part in range(n_part):
                @pl.when(z // n_dest * n_part + part != q)
                def _():
                    arrived(rhs_part(l, part), at(f"Dr{l}").at[part])

        def z_block(l, index):
            return at(f"Z{l}").at[index]

        def c_block(l, index):
            return at(f"C{l}").at[pl.ds(pl.multiple_of(index * K[l], 16), K[l])]

        kinds = {"Z": (inverse, z_block), "C": (coupling, c_block)}

        def start_line(kind, l):
            source, block = kinds[kind]
            src, dst = source[l], block(l, z)
            pltpu.make_async_copy(src, dst, at(f"{kind}r{l}").at[0, 0]).start()
            for way, step in ((0, 1), (1, -1)):
                go_on(kind, l, way, step, 0, src, z)

        def go_on(kind, l, way, step, d, src, origin):
            open_end = jnp.logical_and(z + step >= 0, z + step < R)
            begun = jnp.logical_and(z - d * step >= 0, z - d * step < R)
            ready = jnp.logical_and(open_end, begun)
            dst = kinds[kind][1](l, origin)

            def copy():
                return remote(
                    src, dst, at(f"{kind}s{l}").at[way, d], at(f"{kind}r{l}").at[way, d + 1],
                    (z + step + R) % R, c,
                )

            @pl.when(ready)
            def _():
                copy().start()

            def finish():
                @pl.when(ready)
                def _():
                    copy().wait_send()

            sent.append(finish)

        def pass_line(kind, l, d):
            for way, step in ((0, 1), (1, -1)):
                origin = (z - d * step + R) % R
                block = kinds[kind][1](l, origin)
                begun = jnp.logical_and(z - d * step >= 0, z - d * step < R)

                @pl.when(begun)
                def _():
                    arrived(block, at(f"{kind}r{l}").at[way, d])

                if d < R - 1:
                    go_on(kind, l, way, step, d, block, origin)

        def pass_both(l, d):
            pass_line("Z", l, d)
            if l:
                pass_line("C", l, d)

        def own_line(kind, l):
            arrived(kinds[kind][1](l, z), at(f"{kind}r{l}").at[0, 0])

        def scatter(name, l, landed, ssem, rsem):
            q = c % G[l]
            for m in range(1, G[l]):
                send(
                    at(name).at[flipped(q, m)], at(landed).at[m],
                    at(ssem).at[m], at(rsem).at[m], z, flipped(c, m),
                )

        def total(name, l, landed, rsem):
            value = at(name)[c % G[l]].astype(jnp.float32)
            for m in range(1, G[l]):
                arrived(at(landed).at[m], at(rsem).at[m])
                value = value + at(landed)[m].astype(jnp.float32)
            return value

        def share_solution(l):
            q = c % G[l]
            here = at(f"xs{l}").at[q]
            for m in range(1, G[l]):
                send(here, here, at(f"xss{l}").at[m], at(f"xsr{l}").at[m], z, flipped(c, m))

        def wait_solution(l):
            q = c % G[l]
            for m in range(1, G[l]):
                arrived(at(f"xs{l}").at[flipped(q, m)], at(f"xsr{l}").at[m])

        def share_update(l):
            child, q = (c // G[l]) % 2, c % G[l]
            here = at(f"u{l}").at[child, q]
            for m in range(1, 2 * G[l]):
                send(here, here, at(f"us{l}").at[m], at(f"ur{l}").at[m], z, flipped(c, m))

        def wait_update(l):
            for m in range(1, 2 * G[l]):
                other = flipped(c, m)
                arrived(
                    at(f"u{l}").at[(other // G[l]) % 2, other % G[l]], at(f"ur{l}").at[m]
                )

        def make_table(l):
            front = c // G[l]
            step = K[l]
            for child in range(2):
                row = maps[l + 1][pl.ds(2 * front + child, 1), :]

                def body(i, carry):
                    start = pl.multiple_of(i * step, 16)
                    at_row = lax.broadcasted_iota(jnp.int32, (step, S[l + 1]), 0) + start
                    at(f"hot{l}")[child, pl.ds(start, step), :] = jnp.where(
                        at_row == row, 1.0, 0.0
                    ).astype(bf)
                    return carry

                lax.fori_loop(0, plan.total(l) // step, body, 0)

        def start_out(l):
            q = c % G[l]
            n_dest, n_part = max(1, W[l] // N), max(1, N // W[l])
            if W[l] >= N:
                holds = z // n_dest == q
                index = z % n_dest
                dst = at(f"oT{l}").at[pl.ds(pl.multiple_of(index * N, N), N)]
            else:
                holds = q // n_part == z
                index = 0
                dst = at(f"oT{l}")

            def piece(r):
                if W[l] >= N:
                    return at(f"fx{l}").at[r]
                low = pl.multiple_of((q % n_part) * W[l], W[l])
                return at(f"fx{l}").at[r, pl.ds(low, W[l])]

            def copy_to(d):
                r = (z + d) % R
                return remote(
                    piece(r), dst, at(f"Os{l}").at[d], at(f"Or{l}").at[index], r, c
                )

            @pl.when(holds)
            def _():
                pltpu.make_async_copy(piece(z), dst, at(f"Or{l}").at[index]).start()
                for d in range(1, R):
                    copy_to(d).start()

            def finish():
                @pl.when(holds)
                def _():
                    for d in range(1, R):
                        copy_to(d).wait_send()

            sent.append(finish)

        def finish_out(l):
            if W[l] >= N:
                for i in range(W[l] // N):
                    arrived(at(f"oT{l}").at[pl.ds(i * N, N)], at(f"Or{l}").at[i])
            else:
                arrived(at(f"oT{l}"), at(f"Or{l}").at[0])
            if narrow(W[l]):
                outs[l][...] = at(f"oT{l}")[...]
            else:
                outs[l][...] = dot_nt(eye(K[l]), at(f"oT{l}")[...]).astype(bf)

        def pivot(l, blocks):
            product = dot_nn if narrow(K[l]) else dot_nt
            value = product(blocks[0], at(f"Z{l}")[0])
            for r in range(1, R):
                value = value + product(blocks[r], at(f"Z{l}")[r])
            at(f"y{l}")[...] = value.astype(bf)

        start_line("Z", 3)
        start_line("C", 3)
        start_rhs(3)
        start_line("Z", 2)
        for l in (2, 1, 0):
            start_rhs(l)
        make_table(2)
        pass_both(3, 1)
        start_line("C", 2)
        for d in range(2, R):
            pass_both(3, d)
            if d == 2:
                pass_both(2, 1)
                start_line("Z", 1)
        for l in (2, 1, 0):
            spread_rhs(l)
        spread_rhs(3)
        own_line("Z", 3)
        pivot(3, [at("B3")[r] for r in range(R)])
        own_line("C", 3)
        at("u3")[(c // G[3]) % 2, 0] = (-dot_nt(at("y3")[...], at("C3")[...])).astype(bf)
        share_update(3)
        pass_both(2, 2)
        start_line("C", 1)
        pass_line("Z", 1, 1)
        make_table(1)
        for d in range(3, R):
            pass_both(2, d)

        for l in (2, 1, 0):
            wait_update(l + 1)
            pair = [at(f"u{l + 1}")[child].reshape(N, S[l + 1]) for child in range(2)]

            def assembled(low, size):
                value = dot_nt(pair[0], at(f"hot{l}")[0, low:low + size, :])
                return value + dot_nt(pair[1], at(f"hot{l}")[1, low:low + size, :])

            wait_rhs(l)
            blocks = [
                (at(f"B{l}")[r].astype(jnp.float32) + assembled(r * K[l], K[l])).astype(bf)
                for r in range(R)
            ]
            if l == 1:
                for d in range(3, R):
                    pass_both(1, d)
                pass_line("Z", 0, 2)
            if l == 0:
                for d in range(3, R):
                    pass_line("Z", 0, d)
            own_line("Z", l)
            pivot(l, blocks)
            if l:
                own_line("C", l)
                share = (G[l], N // G[l], S[l])
                at(f"up{l}")[...] = (
                    dot_nt(at(f"y{l}")[...], at(f"C{l}")[...]).astype(bf).reshape(share)
                )
                scatter(f"up{l}", l, f"ut{l}", f"ups{l}", f"upr{l}")
                if l == 2:
                    pass_line("C", 1, 1)
                    start_line("Z", 0)
                    pass_line("Z", 1, 2)
                    make_table(0)
                    pass_line("C", 1, 2)
                    pass_line("Z", 0, 1)
                at(f"H{l}")[...] = assembled(S[l], S[l]).astype(bf).reshape(share)
                reduced = total(f"up{l}", l, f"ut{l}", f"upr{l}")
                q = c % G[l]
                at(f"u{l}")[(c // G[l]) % 2, q] = (
                    at(f"H{l}")[q].astype(jnp.float32) - reduced
                ).astype(bf)
                share_update(l)

        per = G[0] // R
        lanes = S[0] // G[0]
        for r in range(R):
            product = dot_nt if narrow(K[0]) else dot_nn
            value = product(at("y0")[...], at("Z0")[r]).astype(bf)
            for i in range(per):
                at("xp0")[r * per + i] = value[:, i * lanes:(i + 1) * lanes]
        scatter("xp0", 0, "xr0", "xps0", "xpr0")
        at("xs0")[c % G[0]] = total("xp0", 0, "xr0", "xpr0").astype(bf)
        share_solution(0)
        wait_solution(0)
        for r in range(R):
            for i in range(per):
                at("fx0")[r, :, i * lanes:(i + 1) * lanes] = at("xs0")[r * per + i]
        start_out(0)

        for l in (1, 2, 3):
            child = (c // G[l]) % 2
            gathered = dot_nn(at(f"fx{l - 1}")[0], at(f"hot{l - 1}")[child, 0:K[l - 1], :])
            for r in range(1, R):
                gathered = gathered + dot_nn(
                    at(f"fx{l - 1}")[r],
                    at(f"hot{l - 1}")[child, r * K[l - 1]:(r + 1) * K[l - 1], :],
                )
            if l > 1:
                gathered = gathered + dot_nn(
                    at(f"v{l - 1}")[...], at(f"hot{l - 1}")[child, S[l - 1]:, :]
                )
            at(f"v{l}")[...] = gathered.astype(bf)
            residual = (
                at(f"y{l}")[...].astype(jnp.float32)
                - dot_nn(at(f"v{l}")[...], at(f"C{l}")[...])
            ).astype(bf)
            for r in range(R):
                product = dot_nt if narrow(K[l]) else dot_nn
                value = product(residual, at(f"Z{l}")[r]).astype(bf)
                if G[l] > 1:
                    at(f"xp{l}")[:, r] = value.reshape(G[l], N // G[l], K[l])
                else:
                    at(f"fx{l}")[r] = value
            if G[l] > 1:
                if G[l] == 2:
                    send(
                        at(f"xp{l}"), at(f"xr{l}"), at(f"xps{l}").at[1], at(f"xpr{l}").at[1],
                        z, flipped(c, 1),
                    )
                    arrived(at(f"xr{l}"), at(f"xpr{l}").at[1])
                    for r in range(R):
                        both = at(f"xp{l}")[:, r].astype(jnp.float32) + at(f"xr{l}")[:, r].astype(
                            jnp.float32
                        )
                        at(f"fx{l}")[r] = both.astype(bf).reshape(N, K[l])
                    start_out(l)
                    continue
                scatter(f"xp{l}", l, f"xr{l}", f"xps{l}", f"xpr{l}")
                if l == 1:
                    finish_out(0)
                at(f"xs{l}")[c % G[l]] = total(f"xp{l}", l, f"xr{l}", f"xpr{l}").astype(bf)
                share_solution(l)
                wait_solution(l)
                for r in range(R):
                    at(f"fx{l}")[r] = at(f"xs{l}")[:, r].reshape(N, K[l])
            start_out(l)
        for l in (1, 2, 3):
            finish_out(l)
        for finish in sent:
            finish()

    return kernel, scratch


def hand_on(*refs):
    for source, target in zip(refs[:4], refs[4:]):
        target[...] = source[...]


def fused_device(*blocks):
    plan = Plan(
        lax.axis_size("row"), lax.axis_size("col"),
        [block.shape for block in blocks[:4]], blocks[7].shape,
    )
    if not plan.fits():
        return per_device(*blocks)
    kernel, scratch = build_kernel(plan)
    blocks = list(blocks)
    for at in (0, 1, 2, 3, 7, 8, 9, 10):
        if narrow(blocks[at].shape[1]):
            blocks[at] = blocks[at].T
    vmem = pl.BlockSpec(memory_space=pltpu.VMEM)
    solved = pl.pallas_call(
        kernel,
        out_shape=tuple(jax.ShapeDtypeStruct(block.shape, block.dtype) for block in blocks[7:11]),
        in_specs=[vmem] * 14,
        out_specs=(vmem,) * 4,
        scratch_shapes=scratch,
        compiler_params=pltpu.CompilerParams(
            collective_id=0, has_side_effects=True, vmem_limit_bytes=56 * 2**20
        ),
    )(*blocks)
    solved = pl.pallas_call(
        hand_on,
        out_shape=tuple(jax.ShapeDtypeStruct(block.shape, block.dtype) for block in solved),
        in_specs=[vmem] * 4,
        out_specs=(vmem,) * 4,
    )(*solved)
    return tuple(
        block.T if narrow(width) else block for block, width in zip(solved, plan.width)
    )


def solution(mesh):
    in_specs = (
        P("col", "row"),
        P("col", "row"),
        P("col", "row"),
        P("col", "row"),
        P("row", "col"),
        P("row", "col"),
        P("row", "col"),
        P("row", "col"),
        P("row", "col"),
        P("row", "col"),
        P("row", "col"),
        P(),
        P(),
        P(),
    )
    out_specs = (P("row", "col"), P("row", "col"), P("row", "col"), P("row", "col"))
    return jax.shard_map(
        fused_device, mesh=mesh, in_specs=in_specs, out_specs=out_specs, check_vma=False
    )
```

profile of v0, /device:TPU:0, one launch (start us, length us, event | category | flops | bytes accessed | tf_op | source)
XLA Modules:
  0.0 75.4 jit_solution(17391817290574254589)
XLA Ops:
  0.6 73.3 %shard_map.165 = (bf16[32,256]{1,0:T(8,128)(2,1)}, bf16[64,192]{1,0:T(8,128)(2,1)}, bf16[128,128]{1,0:T(8,128)(2,1)}, bf16[64,256]{1,0:T(8,128)(2,1)}) custom-call(bf16[128,256]{1,0:T(8,128)(2,1)} %refs_0_.1, bf16[192,192]{1,0:T(8,128)(2,1)} %refs_1_.1, bf16[256,128]{1,0:T(8,128)(2,1)} %refs_2_.1, bf16[64,256]{1,0:T(8,128)(2,1)} %bitcast.5, ...), custom_call_target="tpu_custom_call" | custom-call | tf_op jit(solution)/shard_map/pallas_call | solution.py:790
  74.0 1.5 %shard_map.166 = (bf16[32,256]{1,0:T(8,128)(2,1)}, bf16[64,192]{1,0:T(8,128)(2,1)}, bf16[128,128]{1,0:T(8,128)(2,1)}, bf16[64,256]{1,0:T(8,128)(2,1)}) custom-call(bf16[32,256]{1,0:T(8,128)(2,1)} %get-tuple-element.12.refs_0_, bf16[64,192]{1,0:T(8,128)(2,1)} %get-tuple-element.13.refs_1_, bf16[128,128]{1,0:T(8,128)(2,1)} %get-tuple-element.14.refs_2_, ...), custom_call_target="tpu_custom_call" | custom-call | tf_op jit(solution)/shard_map/pallas_call | solution.py:800
where the time goes:
time: 75.7 us; the launch traced here: 75.4 us
  Pallas kernels  74.8 us (99%)
    pallas_call x1, Pallas kernels, fused_device(): pl.pallas_call(kernel, out_shape=tuple((jax.ShapeDtypeStruct(block.shape,...  73.3 us

commit v1 on v0

v1 whole, which is shorter than its diff:
```python
import functools

import jax
import jax.numpy as jnp
from jax import lax
from jax.experimental import pallas as pl
from jax.experimental.pallas import tpu as pltpu
from jax.sharding import PartitionSpec as P


def swapped(value, axis, stride):
    mask = 2**stride
    pairs = [(source, source ^ mask) for source in range(lax.axis_size(axis))]
    return lax.ppermute(value, axis, pairs)


def route_tables(mapping, child_index, parent_sep, parent_upd, strips, row_index):
    positions = lax.dynamic_index_in_dim(mapping, child_index, 0, keepdims=False)
    sep_rows = parent_sep // strips
    in_separator = positions < parent_sep
    if parent_upd > 0:
        upd_rows = parent_upd // strips
        target = jnp.where(
            in_separator, positions // sep_rows, (positions - parent_sep) // upd_rows
        )
        offset = jnp.where(
            in_separator, positions % sep_rows, sep_rows + (positions - parent_sep) % upd_rows
        )
    else:
        target = positions // sep_rows
        offset = positions % sep_rows
    block_rows = positions.shape[0] // strips
    blocks = target.reshape(strips, block_rows)
    matches = (blocks[:, :, None] == jnp.arange(strips, dtype=jnp.int32)[None, None, :]).astype(
        jnp.int32
    )
    slot_of = jnp.sum((jnp.cumsum(matches, axis=1) - 1) * matches, axis=2).reshape(-1)
    block_len = sep_rows + parent_upd // strips
    capacity = 2 * positions.shape[0] // (strips * strips)
    source = jnp.arange(positions.shape[0], dtype=jnp.int32) // block_rows
    mine_here = target == row_index
    column_at = jnp.where(mine_here, slot_of, capacity)
    lookup = jnp.full((strips, capacity + 1), block_len, jnp.int32)
    lookup = lookup.at[source, column_at].set(jnp.where(mine_here, offset, block_len))[:, :capacity]
    local_target = lax.dynamic_slice_in_dim(target, row_index * block_rows, block_rows)
    local_slots = lax.dynamic_slice_in_dim(slot_of, row_index * block_rows, block_rows)
    return (local_target, local_slots, lookup, capacity, block_len)


def pack_rows(values, local_target, local_slots, strips, capacity):
    buffer = jnp.zeros((strips, capacity, values.shape[1]), values.dtype)
    return buffer.at[local_target, local_slots].set(values)


def unpack_rows(received, lookup, block_len):
    summed = jnp.zeros((block_len + 1, received.shape[2]), jnp.float32)
    return summed.at[lookup].add(received.astype(jnp.float32))[:block_len]


def spread(portion, depth_bits, pass_on, column):
    for bit_index in range(depth_bits):
        partner = pass_on(portion, bit_index)
        is_upper = column >> bit_index & 1 == 1
        portion = jnp.where(
            is_upper,
            jnp.concatenate([partner, portion], axis=-1),
            jnp.concatenate([portion, partner], axis=-1),
        )
    return portion


def shrink(entire, depth_bits, pass_on, column):
    for bit_index in reversed(range(depth_bits)):
        half_width = entire.shape[-1] // 2
        low_part = entire[..., :half_width]
        high_part = entire[..., half_width:]
        is_upper = column >> bit_index & 1 == 1
        kept_part = jnp.where(is_upper, high_part, low_part)
        sent_part = jnp.where(is_upper, low_part, high_part)
        entire = kept_part + pass_on(sent_part, bit_index)
    return entire


def per_device(
    inverse_top,
    inverse_one,
    inverse_two,
    inverse_leaf,
    coupling_one,
    coupling_two,
    coupling_leaf,
    rhs_top,
    rhs_one,
    rhs_two,
    rhs_leaf,
    parent_map_one,
    parent_map_two,
    parent_map_leaf,
):
    strips = lax.axis_size("row")
    col_count = lax.axis_size("col")
    row_here = lax.axis_index("row")
    column = lax.axis_index("col")
    inverses = [inverse_top, inverse_one, inverse_two, inverse_leaf]
    couplings = [None, coupling_one, coupling_two, coupling_leaf]
    right_sides = [rhs_top, rhs_one, rhs_two, rhs_leaf]
    parent_maps = [None, parent_map_one, parent_map_two, parent_map_leaf]
    orders = [inverse.shape[1] * strips for inverse in inverses]
    groups = [col_count >> tree_level for tree_level in range(4)]
    group_bits = [group_size.bit_length() - 1 for group_size in groups]
    pass_rhs = lambda values, bit_index: swapped(values, "col", bit_index)
    pass_update_sum = lambda values, bit_index: swapped(
        values.astype(jnp.bfloat16), "col", bit_index
    ).astype(values.dtype)
    pass_update_spread = lambda values, bit_index: swapped(values, "col", bit_index)
    pass_solution_sum = lambda values, bit_index: swapped(
        values.astype(jnp.bfloat16), "col", bit_index
    ).astype(values.dtype)
    pass_solution_spread = lambda values, bit_index: swapped(values, "col", bit_index)
    full_rhs = [
        spread(right_sides[tree_level], group_bits[tree_level], pass_rhs, column)
        for tree_level in range(4)
    ]
    own_routes = [None]
    for tree_level in range(1, 4):
        parent_order = orders[tree_level - 1]
        parent_update = parent_order if tree_level > 1 else 0
        front_here = column // groups[tree_level]
        own_routes.append(
            route_tables(
                parent_maps[tree_level], front_here, parent_order, parent_update, strips, row_here
            )
        )
    pivots = [None] * 4
    incoming = None
    for tree_level in (3, 2, 1, 0):
        sep_rows = inverses[tree_level].shape[1]
        if incoming is None:
            separator = full_rhs[tree_level]
            own_update = None
        else:
            separator = (full_rhs[tree_level].astype(jnp.float32) + incoming[:sep_rows]).astype(
                jnp.bfloat16
            )
            own_update = lax.optimization_barrier(incoming[sep_rows:].astype(jnp.bfloat16))
        partial_value = jnp.dot(inverses[tree_level], separator, preferred_element_type=jnp.float32)
        solved = lax.psum(partial_value.astype(jnp.bfloat16), "row")
        pivots[tree_level] = solved
        if tree_level > 0:
            coupled = jnp.dot(couplings[tree_level], solved, preferred_element_type=jnp.float32)
            reduced = shrink(coupled, group_bits[tree_level], pass_update_sum, column)
            if own_update is None:
                portion = (-reduced).astype(jnp.bfloat16)
            else:
                start_at = column % groups[tree_level] * reduced.shape[1]
                kept_rows = lax.dynamic_slice_in_dim(own_update, start_at, reduced.shape[1], 1)
                portion = (kept_rows.astype(jnp.float32) - reduced).astype(jnp.bfloat16)
            updated = spread(portion, group_bits[tree_level], pass_update_spread, column)
            own_target, own_slots, own_lookup, capacity, block_len = own_routes[tree_level]
            got_own = lax.all_to_all(
                pack_rows(updated, own_target, own_slots, strips, capacity),
                "row",
                split_axis=0,
                concat_axis=0,
                tiled=True,
            )
            own_part = unpack_rows(got_own, own_lookup, block_len)
            partner = swapped(own_part.astype(jnp.bfloat16), "col", group_bits[tree_level])
            incoming = own_part + partner.astype(jnp.float32)
    solutions = [None] * 4
    parent_solution = None
    parent_gathered = None
    for tree_level in range(4):
        solved = pivots[tree_level]
        gathered = None
        if tree_level == 0:
            residual = solved
        else:
            own_target, own_slots, own_lookup, capacity, block_len = own_routes[tree_level]
            pieces = [parent_solution]
            if parent_gathered is not None:
                pieces.append(parent_gathered)
            pieces.append(jnp.zeros((1, parent_solution.shape[1]), jnp.bfloat16))
            parent_rows = jnp.concatenate(pieces, axis=0)
            returned = lax.all_to_all(
                parent_rows[own_lookup], "row", split_axis=0, concat_axis=0, tiled=True
            )
            gathered = returned[own_target, own_slots]
            coupling_term = jnp.dot(
                couplings[tree_level].T, gathered, preferred_element_type=jnp.float32
            )
            residual = (
                solved.astype(jnp.float32)
                - lax.psum(coupling_term.astype(jnp.bfloat16), "row").astype(jnp.float32)
            ).astype(jnp.bfloat16)
        contribution = jnp.dot(inverses[tree_level].T, residual, preferred_element_type=jnp.float32)
        if tree_level == 0:
            summed = lax.psum(contribution.astype(jnp.bfloat16), "col")
            solution = summed
            rhs_width = solution.shape[1] // groups[0]
            solutions[0] = lax.dynamic_slice_in_dim(
                solution, column % groups[0] * rhs_width, rhs_width, 1
            )
        else:
            portion = shrink(
                contribution, group_bits[tree_level], pass_solution_sum, column
            ).astype(jnp.bfloat16)
            solutions[tree_level] = portion
            if tree_level < 3:
                solution = spread(portion, group_bits[tree_level], pass_solution_spread, column)
        parent_solution = solution
        parent_gathered = gathered
    return (solutions[0], solutions[1], solutions[2], solutions[3])


MESH = pl.DeviceIdType.MESH
VMEM_LIMIT = 56 * 2**20


def dot_nn(left, right):
    return lax.dot_general(left, right, (((1,), (0,)), ((), ())), preferred_element_type=jnp.float32)


def dot_nt(left, right):
    return lax.dot_general(left, right, (((1,), (1,)), ((), ())), preferred_element_type=jnp.float32)


def eye(size):
    rows = lax.broadcasted_iota(jnp.int32, (size, size), 0)
    columns = lax.broadcasted_iota(jnp.int32, (size, size), 1)
    return jnp.where(rows == columns, 1.0, 0.0).astype(jnp.bfloat16)


def flipped(value, mask):
    result = value
    bit = 1
    while bit <= mask:
        if mask & bit:
            result = result + bit * (1 - 2 * ((value // bit) % 2))
        bit *= 2
    return result


class Plan:
    def __init__(self, rows, cols, inverse_shapes, rhs_top_shape, map_shape):
        self.rows, self.cols = rows, cols
        self.strip = [shape[1] for shape in inverse_shapes]
        self.order = [shape[1] * rows for shape in inverse_shapes]
        self.local = [shape[0] for shape in inverse_shapes]
        self.group = [cols >> level for level in range(4)]
        self.columns = rhs_top_shape[1] * cols
        self.width = [self.columns // group if group else 0 for group in self.group]
        self.mine = self.columns // rows
        self.map_shape = map_shape

    def total(self, level):
        return self.order[level] * (2 if level else 1)

    def span_rows(self):
        n, order, width = self.mine, self.order, self.width
        shared = 7 * (n // 4) * order[1] + 10 * (n // 2) * (order[0] // 4) + n // 2 * order[1]
        inner = 2 * n * order[3] + 4 * n * order[2] + 7 * (n // 4) * order[1]
        return max(shared, inner, 7 * width[0] * order[0], 3 * n * order[2]) // 128

    def fits(self):
        table = sum(
            2 * self.total(level) * self.order[level + 1] * 2 for level in range(3)
        )
        if self.rows != 4 or self.group[3] != 1 or self.mine * self.rows != self.columns or table > 24 * 2**20:
            return False
        if self.group != [8, 4, 2, 1] or self.mine % 64:
            return False
        for level in range(4):
            if self.strip[level] % 64 or self.order[level] % 128 or self.local[level] % 64:
                return False
        if not packed((self.mine, self.strip[1])):
            return False
        return narrow(self.strip[3]) and not any(narrow(strip) for strip in self.strip[:3])


def elements(shape):
    count = 1
    for extent in shape:
        count *= extent
    return count


def packed(shape):
    return shape[1] > 128 and shape[1] % 128 == 64


def packed_shape(shape):
    return (shape[0] * (shape[1] // 128) + shape[0] // 2, 128)


def narrow(size):
    return size < 128


def phase(number):
    return jax.named_scope(str(number))


def build_kernel(plan):
    R, CC, N = plan.rows, plan.cols, plan.mine
    S, K, L, G, W = plan.order, plan.strip, plan.local, plan.group, plan.width
    N2, NH, NQ, chips = 2 * N, N // 2, N // G[1], G[0] // 2
    bf = jnp.bfloat16
    scratch = []

    def ref(shape, dtype=bf):
        scratch.append(pltpu.VMEM(shape, dtype))
        return len(scratch) - 1

    def sems(*shape):
        scratch.append(pltpu.SemaphoreType.DMA(shape) if shape else pltpu.SemaphoreType.DMA)
        return len(scratch) - 1

    levels, lower = range(4), (1, 2, 3)
    z_shape = [(S[3], L[3]) if l == 3 else (L[l], S[l]) for l in levels]
    c_shape = [None] + [(S[l], L[l]) for l in lower]
    Z = [ref(z_shape[l]) for l in levels]
    C = [None] + [ref(c_shape[l]) for l in lower]
    Zm = [None] + [ref(z_shape[l]) for l in lower]
    Cm = [None] + [ref(c_shape[l]) for l in lower]
    Zp = [ref((R,) + packed_shape((L[l], K[l]))) if l < 3 and packed((L[l], K[l])) else None for l in levels]
    Cp = [None] + [ref((R,) + packed_shape((K[l], L[l]))) if packed((K[l], L[l])) else None for l in lower]
    Zraw = [ref((L[l], K[l])) if Zp[l] is not None else None for l in levels]
    Craw = [None] + [ref((K[l], L[l])) if Cp[l] is not None else None for l in lower]
    Zr, Zs = [sems(R) for _ in levels], [sems() for _ in levels]
    Cr, Cs = [sems(R) for _ in levels], [sems() for _ in levels]
    Zmr, Zms = [sems() for _ in levels], [sems() for _ in levels]
    Cmr, Cms = [sems() for _ in levels], [sems() for _ in levels]
    table = [ref((2, plan.total(l), S[l + 1])) for l in range(3)]
    held_map = [None] + [ref(plan.map_shape[l - 1], jnp.int32) for l in lower]
    local = sems(8)
    B = [ref((N, S[0])), ref((2, R) + packed_shape((N, K[1]))), ref((S[2], N2)), ref((S[3], N2))]
    B1, rhs_raw, rhs_packed = ref((N2, S[1])), ref((N, K[1])), ref(packed_shape((N, K[1])))
    Bs, Br = [sems() for _ in levels], [sems() for _ in levels]
    Ds, Dr = [sems(), sems(G[1]), sems()], [sems(2), sems(2), sems()]
    y = [ref((N, L[0]))] + [ref((4, NH, L[l])) for l in lower]
    yb = [None] + [ref((2, NH, L[l])) for l in lower]
    ys, yr = [sems() for _ in levels], [sems() for _ in levels]
    u = [None, ref((2, G[1], NQ, S[1])), ref((2, 2, G[1], NQ, S[2])), ref((2, N2, S[3]))]
    ur = [sems() for _ in levels]
    up1, ut1, ut1r = ref((2, G[1], NQ, S[1])), ref((G[1], NQ, S[1])), sems()
    h1 = ref((2, NQ, S[1]))
    up2, ut2, ut2r = ref((2, N, S[2])), ref((N, S[2])), sems()
    xp0, xr0, xr0r = ref((chips, 2, NH, S[0] // chips)), ref((CC, NH, S[0] // chips)), sems()
    xs0, xs0r = ref((chips, NH, S[0] // chips)), sems()
    xp1, xr1, xr1r = ref((NH, S[1])), ref((NH, S[1])), sems()
    v = [None] + [ref((NH, S[l])) for l in (1, 2)]
    x1, x2 = ref((NH, S[1])), ref((NH, S[2]))
    f1, f3 = ref((R, NH, K[1])), ref((2 * R, NH, K[3]))
    Os, Or = [sems() for _ in levels], [sems() for _ in levels]
    plane, inner = sems(), sems()
    span = ref((plan.span_rows(), 128))

    def kernel(*refs):
        inverse = refs[0:4]
        coupling = (None,) + tuple(refs[4:7])
        rhs = refs[7:11]
        maps = (None,) + tuple(refs[11:14])
        outs = refs[14:18]
        held = refs[18:]
        at = lambda index: held[index]
        z = lax.axis_index("row")
        c = lax.axis_index("col")
        core, chip = c % 2, c // 2
        middle = jnp.logical_and(z > 0, z < R - 1)
        border = jnp.logical_not(middle)
        half = z % 2
        pair = z + 1 - 2 * half
        across = R - 1 - z
        beyond = R - 1 - pair
        sent = {}

        def remote(src, dst, ssem, rsem, z_to, c_to):
            return pltpu.make_async_remote_copy(
                src_ref=src, dst_ref=dst, send_sem=ssem, recv_sem=rsem,
                device_id=(z_to, c_to), device_id_type=MESH,
            )

        def push(src, dst, ssem, rsem, z_to, c_to):
            remote(src, dst, ssem, rsem, z_to, c_to).start()

        def counted(src, dst, index, rsem, z_to, c_to):
            push(src, dst, at(index), rsem, z_to, c_to)
            sent[index] = sent.get(index, 0) + elements(src.shape)

        def arrived(dst, rsem):
            pltpu.make_async_copy(dst, dst, rsem).wait()

        def take(sem, count):
            view = at(span).at[pl.ds(0, count // 128)]
            pltpu.make_async_copy(view, view, sem).wait()

        barrier = pltpu.get_barrier_semaphore()
        friends = [(z, flipped(c, m)) for m in range(1, CC)]
        for d in range(1, R):
            friends += [((z + d) % R, c), ((z + d) % R, flipped(c, 1))]
        friends += [(pair, flipped(c, m)) for m in range(2, G[1])]
        for friend in friends:
            pl.semaphore_signal(barrier, inc=1, device_id=friend, device_id_type=MESH)

        raws = []
        for l in levels:
            if Zp[l] is not None:
                raws.append((inverse[l], at(Zraw[l])))
            if l and Cp[l] is not None:
                raws.append((coupling[l], at(Craw[l])))
        raws.append((rhs[1], at(rhs_raw)))
        loads = raws + [(maps[l], at(held_map[l])) for l in lower]
        for i, (src, dst) in enumerate(loads):
            pltpu.make_async_copy(src, dst, at(local).at[i]).start()

        def slot(kind, l, r):
            if kind == 0:
                if Zp[l] is not None:
                    return at(Zp[l]).at[r], at(Zr[l]).at[r]
                if l == 3:
                    low = pl.multiple_of(r * K[l], 16)
                    return at(Z[l]).at[pl.ds(low, K[l])], at(Zr[l]).at[r]
                low = pl.multiple_of(r * K[l], 128)
                return at(Z[l]).at[:, pl.ds(low, K[l])], at(Zr[l]).at[r]
            if Cp[l] is not None:
                return at(Cp[l]).at[r], at(Cr[l]).at[r]
            low = pl.multiple_of(r * K[l], 16)
            return at(C[l]).at[pl.ds(low, K[l])], at(Cr[l]).at[r]

        def is_packed(kind, l):
            return (Zp, Cp)[kind][l] is not None

        def source(kind, l):
            if is_packed(kind, l):
                return slot(kind, l, z)[0]
            return (inverse, coupling)[kind][l]

        def send_sem(kind, l):
            return at((Zs, Cs)[kind][l])

        def own_load(kind, l):
            if not is_packed(kind, l):
                dst, sem = slot(kind, l, z)
                pltpu.make_async_copy(source(kind, l), dst, sem).start()

        def own_send(kind, l):
            dst, sem = slot(kind, l, z)
            push(source(kind, l), dst, send_sem(kind, l), sem, jnp.where(middle, across, pair), c)

            @pl.when(border)
            def _():
                push(source(kind, l), dst, send_sem(kind, l), sem, beyond, c)

        def own_out(kind, l):
            dst, sem = slot(kind, l, z)
            push(source(kind, l), dst, send_sem(kind, l), sem, pair, c)

        def pass_on(kind, l):
            for r in (across, beyond):
                dst, sem = slot(kind, l, r)
                push(dst, dst, send_sem(kind, l), sem, pair, c)

        def settle(kind, l, which):
            for r in which:
                arrived(*slot(kind, l, r))

        def settle_all(kind, l):
            settle(kind, l, (pair, across, beyond) if is_packed(kind, l) else (z, pair, across, beyond))
            if is_packed(kind, l):
                unpack(kind, l)

        def unpacked(block, rows, lanes):
            whole = lanes // 128 * rows
            rest = block[whole:]
            rest = jnp.concatenate([rest[:, :lanes % 128], rest[:, lanes % 128:]], axis=0)
            return jnp.concatenate([block[i:i + rows] for i in range(0, whole, rows)] + [rest], axis=1)

        def unpack(kind, l):
            rows, lanes = (L[l], K[l]) if kind == 0 else (K[l], L[l])
            for r in range(R):
                value = unpacked(at((Zp, Cp)[kind][l])[r], rows, lanes)
                if kind == 0:
                    at(Z[l])[:, r * lanes:(r + 1) * lanes] = value
                else:
                    at(C[l])[r * rows:(r + 1) * rows, :] = value

        def pack(raw):
            value = raw[...]
            rows, lanes = value.shape
            whole = lanes - lanes % 128
            pieces = [value[:, i:i + 128] for i in range(0, whole, 128)]
            rest = value[:, whole:]
            rest = jnp.concatenate([rest[:rows // 2], rest[rows // 2:]], axis=1)
            return jnp.concatenate(pieces + [rest], axis=0)

        def drain(kind, l):
            if is_packed(kind, l):
                whole = at((Zp, Cp)[kind][l])
                part = whole.at[pl.ds(0, R // 2)]
            else:
                whole = at((Z, C)[kind][l])
                if kind == 0 and l < 3:
                    part = whole.at[:, pl.ds(0, S[l] // 2)]
                else:
                    part = whole.at[pl.ds(0, S[l] // 2)]

            @pl.when(middle)
            def _():
                arrived(whole, send_sem(kind, l))

            @pl.when(border)
            def _():
                arrived(part, send_sem(kind, l))

        def rhs_pieces(l):
            q = c % G[l]
            if l == 3:
                return [
                    (rhs[3].at[:, pl.ds(i * N2, N2)], at(B[3]).at[pl.ds(pl.multiple_of(z * K[3], 16), K[3])], 1 + i)
                    for i in range(2)
                ]
            if l == 2:
                return [(rhs[2], at(B[2]).at[pl.ds(pl.multiple_of(z * K[2], 16), K[2])], 1 + q)]
            if l == 1:
                return [(at(rhs_packed), at(B[1]).at[q % 2, z], 1 + q // 2)]
            rows = pl.ds(pl.multiple_of((q % 2) * W[0], W[0]), W[0])
            lanes = pl.ds(pl.multiple_of(z * K[0], 128), K[0])
            return [(rhs[0], at(B[0]).at[rows, lanes], q // 2)]

        def start_rhs(l):
            for src, dst, z_to in rhs_pieces(l):
                @pl.when(z_to == z)
                def _():
                    pltpu.make_async_copy(src, dst, at(Br[l])).start()

                @pl.when(z_to != z)
                def _():
                    push(src, dst, at(Bs[l]), at(Br[l]), z_to, c)

        def drain_rhs(l):
            pieces = rhs_pieces(l)
            if l == 3:
                @pl.when(middle)
                def _():
                    arrived(at(B[3]).at[pl.ds(0, K[3])], at(Bs[3]))

                @pl.when(border)
                def _():
                    arrived(at(B[3]).at[pl.ds(0, 2 * K[3])], at(Bs[3]))
                return
            src, dst, z_to = pieces[0]

            @pl.when(z_to != z)
            def _():
                arrived(dst, at(Bs[l]))

        def rhs_spread(l):
            q = c % G[l]
            if l == 2:
                return z == 1 + q, at(B[2]), at(Dr[2])
            if l == 1:
                return z == 1 + q // 2, at(B[1]).at[q % 2], at(Dr[1]).at[q % 2]
            rows = pl.ds(pl.multiple_of((q % 2) * W[0], W[0]), W[0])
            return z == q // 2, at(B[0]).at[rows], at(Dr[0]).at[q % 2]

        def spread_rhs(l):
            holds, here, rsem = rhs_spread(l)

            @pl.when(holds)
            def _():
                arrived(here, at(Br[l]))
                for m in range(1, G[l]):
                    ssem = at(Ds[l]).at[m] if l == 1 else at(Ds[l])
                    push(here, here, ssem, rsem, z, flipped(c, m))

        def drain_spread(l):
            holds, here, _ = rhs_spread(l)

            @pl.when(holds)
            def _():
                if l == 1:
                    for m in range(1, G[l]):
                        arrived(here, at(Ds[l]).at[m])
                else:
                    take(at(Ds[l]), (G[l] - 1) * elements(here.shape))

        def wait_rhs(l):
            holds, here, rsem = rhs_spread(l)
            if l == 2:
                @pl.when(jnp.logical_not(holds))
                def _():
                    arrived(here, rsem)
                return
            for part in range(2):
                @pl.when(jnp.logical_not(jnp.logical_and(holds, c % 2 == part)))
                def _():
                    view = at(B[1]).at[part] if l == 1 else at(B[0]).at[pl.ds(part * W[0], W[0])]
                    arrived(view, at(Dr[l]).at[part])

        def make_table(l):
            front = c // G[l]
            step = K[l]
            for child in range(2):
                row = at(held_map[l + 1])[pl.ds(2 * front + child, 1), :]

                def body(i, carry):
                    start = pl.multiple_of(i * step, 16)
                    at_row = lax.broadcasted_iota(jnp.int32, (step, S[l + 1]), 0) + start
                    at(table[l])[child, pl.ds(start, step), :] = jnp.where(
                        at_row == row, 1.0, 0.0
                    ).astype(bf)
                    return carry

                lax.fori_loop(0, plan.total(l) // step, body, 0)

        def gathered(l, low, size, first, second):
            value = dot_nt(first, at(table[l])[0, low:low + size, :])
            return value + dot_nt(second, at(table[l])[1, low:low + size, :])

        def forward(kind, l):
            own, copy = at((Z, C)[kind][l]), at((Zm, Cm)[kind][l])
            push(
                own, copy, at((Zms, Cms)[kind][l]), at((Zmr, Cmr)[kind][l]), z, flipped(c, 1)
            )

        with phase(1):
            for i, (src, dst) in enumerate(loads):
                pltpu.make_async_copy(src, dst, at(local).at[i]).wait()
            for l in levels:
                if Zp[l] is not None:
                    at(Zp[l])[z] = pack(at(Zraw[l]))
                if l and Cp[l] is not None:
                    at(Cp[l])[z] = pack(at(Craw[l]))
            at(rhs_packed)[...] = pack(at(rhs_raw))
        with phase(2):
            pl.semaphore_wait(barrier, len(friends))

        with phase(3):
            own_send(0, 3)
            start_rhs(3)
            own_send(1, 3)
            for l in (2, 1, 0):
                start_rhs(l)
            own_send(0, 2)
            own_send(1, 2)
            own_send(0, 1)
            own_send(1, 1)
            own_send(0, 0)
            for l in levels:
                own_load(0, l)
                if l:
                    own_load(1, l)

            @pl.when(middle)
            def _():
                own_out(0, 0)
                for l in (3, 2, 1):
                    own_out(0, l)
                    own_out(1, l)
        make_table(2)

        @pl.when(middle)
        def _():
            with phase(31):
                arrived(at(B[3]), at(Br[3]))
                right = dot_nt(eye(N2), at(B[3])[...]).astype(bf)
                settle_all(0, 3)
            with phase(32):
                solved = dot_nn(right, at(Z[3])[...]).astype(bf)
                at(y[3])[...] = solved.reshape(4, NH, L[3])
                settle_all(1, 3)
            with phase(33):
                at(u[3])[core] = (-dot_nt(solved, at(C[3])[...])).astype(bf)
                here = at(u[3]).at[core]
                counted(here, here, inner, at(ur[3]), z, flipped(c, 1))
                pass_on(0, 3)
                pass_on(1, 3)
        for l in (2, 1, 0):
            spread_rhs(l)
        make_table(1)

        @pl.when(middle)
        def _():
            with phase(21):
                arrived(at(u[3]).at[0], at(ur[3]))
                wait_rhs(2)
            with phase(22):
                pair_of = at(u[3])[0], at(u[3])[1]
                right = dot_nt(eye(N2), at(B[2])[...]) + gathered(2, 0, S[2], *pair_of)
                right = right.astype(bf)
                lower_part = pl.ds(pl.multiple_of(core * N, N), N)
                pair_of = at(u[3])[0, lower_part, :], at(u[3])[1, lower_part, :]
                kept = gathered(2, S[2], S[2], *pair_of)
            with phase(23):
                settle_all(0, 2)
                pass_on(0, 2)
            with phase(24):
                solved = dot_nt(right, at(Z[2])[...]).astype(bf)
                at(y[2])[...] = solved.reshape(4, NH, L[2])
            with phase(25):
                settle_all(1, 2)
                pass_on(1, 2)
            with phase(26):
                at(up2)[...] = dot_nt(solved, at(C[2])[...]).astype(bf).reshape(2, N, S[2])
                counted(at(up2).at[1 - core], at(ut2), inner, at(ut2r), z, flipped(c, 1))
            with phase(27):
                own = at(up2)[core].astype(jnp.float32)
                arrived(at(ut2), at(ut2r))
                own = kept - (own + at(ut2)[...].astype(jnp.float32))
                child = (c // G[2]) % 2
                at(u[2])[child, core] = own.astype(bf).reshape(G[1], NQ, S[2])
                here = at(u[2]).at[child, core]
                for m in range(1, G[1]):
                    counted(here, here, inner, at(ur[2]), z, flipped(c, m))
        make_table(0)
        q, child = c % G[1], (c // G[1]) % 2

        @pl.when(middle)
        def _():
            with phase(11):
                wait_rhs(1)
                for part in range(2):
                    for r in range(R):
                        value = unpacked(at(B[1])[part, r], N, K[1])
                        at(B1)[part * N:(part + 1) * N, r * K[1]:(r + 1) * K[1]] = value
            with phase(12):
                take(at(ur[2]), 3 * N * S[2])
            with phase(13):
                pair_of = [at(u[2])[i].reshape(N2, S[2]) for i in range(2)]
                right = at(B1)[...].astype(jnp.float32) + gathered(1, 0, S[1], *pair_of)
                right = right.astype(bf)
                pair_of = [at(u[2])[i, :, q].reshape(2 * NQ, S[2]) for i in range(2)]
                kept = gathered(1, S[1], S[1], *pair_of)
                at(h1)[...] = kept.astype(bf).reshape(2, NQ, S[1])
            with phase(14):
                settle_all(0, 1)
            with phase(15):
                solved = dot_nt(right, at(Z[1])[...]).astype(bf)
                at(y[1])[...] = solved.reshape(4, NH, L[1])
            with phase(16):
                settle_all(1, 1)
            with phase(17):
                coupled = dot_nt(solved, at(C[1])[...])
                at(up1)[...] = coupled.astype(bf).reshape(2, G[1], NQ, S[1])
                at(up1)[1 - half, q] = (
                    at(up1)[1 - half, q].astype(jnp.float32) - at(h1)[1 - half].astype(jnp.float32)
                ).astype(bf)
                for m in range(G[1]):
                    src = at(up1).at[1 - half, flipped(q, m)]
                    counted(src, at(ut1).at[m], inner, at(ut1r), pair, flipped(c, m))
                for m in range(1, G[1]):
                    src = at(up1).at[half, flipped(q, m)]
                    counted(src, at(ut1).at[m], inner, at(ut1r), z, flipped(c, m))

        @pl.when(border)
        def _():
            with phase(18):
                for l in (3, 2):
                    for kind in range(2):
                        settle_all(kind, l)
                        forward(kind, l)
                arrived(at(ut1), at(ut1r))
                value = at(ut1)[0].astype(jnp.float32)
                for m in range(1, G[1]):
                    value = value + at(ut1)[m].astype(jnp.float32)
                at(u[1])[child, q] = (-value).astype(bf)

        @pl.when(middle)
        def _():
            with phase(19):
                value = at(up1)[half, q].astype(jnp.float32)
                arrived(at(ut1).at[pl.ds(1, G[1] - 1)], at(ut1r))
                for m in range(1, G[1]):
                    value = value + at(ut1)[m].astype(jnp.float32)
                at(u[1])[child, q] = (at(h1)[half].astype(jnp.float32) - value).astype(bf)
        here = at(u[1]).at[child, q]
        for m in range(1, CC):
            counted(here, here, plane, at(ur[1]), z, flipped(c, m))

        @pl.when(middle)
        def _():
            with phase(20):
                for l in lower:
                    at(yb[l])[0] = at(y[l])[2 * half + core]
                    src = at(y[l]).at[2 * half + 1 - core]
                    push(src, at(yb[l]).at[1], at(ys[l]), at(yr[l]), z, flipped(c, 1))
                    src = at(y[l]).at[2 * (1 - half) + core]
                    push(src, at(yb[l]).at[0], at(ys[l]), at(yr[l]), pair, c)
                    src = at(y[l]).at[2 * (1 - half) + 1 - core]
                    push(src, at(yb[l]).at[1], at(ys[l]), at(yr[l]), pair, flipped(c, 1))
                for l in lower:
                    for kind in range(2):
                        forward(kind, l)
                settle(0, 0, (across, beyond))
                pass_on(0, 0)
                pass_on(0, 1)
                pass_on(1, 1)
        with phase(41):
            take(at(ur[1]), (CC - 1) * NQ * S[1])
            wait_rhs(0)
        with phase(42):
            pair_of = [at(u[1])[i].reshape(N, S[1]) for i in range(2)]
            right = at(B[0])[...].astype(jnp.float32) + gathered(0, 0, S[0], *pair_of)
            right = right.astype(bf)
        with phase(43):
            settle(0, 0, (z, pair))

            @pl.when(border)
            def _():
                settle(0, 0, (across, beyond))
        with phase(44):
            solved = dot_nt(right, at(Z[0])[...]).astype(bf)
            value = dot_nn(solved, at(Z[0])[...]).astype(bf)
            wide = S[0] // chips
            for j in range(chips):
                at(xp0)[j] = value[:, j * wide:(j + 1) * wide].reshape(2, NH, wide)
            for m in range(1, CC):
                to = flipped(c, m)
                counted(at(xp0).at[to // 2, to % 2], at(xr0).at[m], plane, at(xr0r), z, to)

        @pl.when(border)
        def _():
            with phase(45):
                for kind in range(2):
                    settle_all(kind, 1)
                    forward(kind, 1)
        with phase(46):
            value = at(xp0)[chip, core].astype(jnp.float32)
            arrived(at(xr0).at[pl.ds(1, CC - 1)], at(xr0r))
            for m in range(1, CC):
                value = value + at(xr0)[m].astype(jnp.float32)
            at(xs0)[chip] = value.astype(bf)
            here = at(xs0).at[chip]
            for m in range(2, CC, 2):
                counted(here, here, plane, at(xs0r), z, flipped(c, m))
        with phase(47):
            arrived(at(xs0).at[pl.ds(1, chips - 1)], at(xs0r))

        def leave(l, piece, dst, c_to):
            @pl.when(c_to == c)
            def _():
                pltpu.make_async_copy(piece(z), dst, at(Or[l])).start()

            @pl.when(c_to != c)
            def _():
                push(piece(z), dst, at(Os[l]), at(Or[l]), z, c_to)
            for d in (2, 1, 3):
                r = (z + d) % R
                push(piece(r), dst, at(Os[l]), at(Or[l]), r, c_to)

        top_here, one_here = chip == z, q // 2 == z // 2
        one_to, two_to = 2 * chip + z % 2, 2 * chip + z // 2

        @pl.when(top_here)
        def _():
            leave(0, lambda r: at(xs0).at[r], outs[0], c)

        def placed(l, low):
            return outs[l].at[pl.ds(pl.multiple_of(low, 16), NH)]

        with phase(51):
            value = None
            for r in range(chips):
                part = dot_nn(at(xs0)[r], at(table[0])[child, r * wide:(r + 1) * wide, :])
                value = part if value is None else value + part
            at(v[1])[...] = value.astype(bf)
            low = at(v[1])[...]

        def residual(l, index, coupled, low):
            return (at(yb[l])[index].astype(jnp.float32) - dot_nn(low, at(coupled[l])[...])).astype(bf)

        def wait_mate(l):
            @pl.when(middle)
            def _():
                arrived(at(yb[l]).at[1], at(yr[l]))

            @pl.when(border)
            def _():
                arrived(at(yb[l]), at(yr[l]))
            arrived(at(Zm[l]), at(Zmr[l]))
            arrived(at(Cm[l]), at(Cmr[l]))

        with phase(52):
            wait_mate(1)
        with phase(53):
            value = dot_nn(residual(1, 0, C, low), at(Z[1])[...])
            value = value + dot_nn(residual(1, 1, Cm, low), at(Zm[1])[...])
            at(xp1)[...] = value.astype(bf)
            counted(at(xp1), at(xr1), plane, at(xr1r), z, flipped(c, 2))
        side = chip % 2
        with phase(54):
            early = dot_nn(low, at(table[1])[side, S[1]:, :])
            arrived(at(xr1), at(xr1r))
        with phase(55):
            value = (at(xp1)[...].astype(jnp.float32) + at(xr1)[...].astype(jnp.float32)).astype(bf)
            at(v[2])[...] = (dot_nn(value, at(table[1])[side, :S[1], :]) + early).astype(bf)
            at(x1)[...] = value
            low = at(v[2])[...]
        with phase(56):
            wait_mate(2)
        with phase(57):
            value = dot_nn(residual(2, 0, C, low), at(Z[2])[...])
            value = value + dot_nn(residual(2, 1, Cm, low), at(Zm[2])[...])
            at(x2)[...] = value.astype(bf)
            high = at(x2)[...]
        with phase(58):
            @pl.when(one_here)
            def _():
                for r in range(R):
                    at(f1)[r] = at(x1)[:, r * K[1]:(r + 1) * K[1]]
                leave(1, lambda r: at(f1).at[r], placed(1, core * NH), one_to)

            def two_piece(r):
                return at(x2).at[:, pl.ds(pl.multiple_of(r * K[2], 128), K[2])]

            leave(2, two_piece, placed(2, half * N + core * NH), two_to)
        with phase(59):
            wait_mate(3)
        with phase(60):
            for mate in range(2):
                leaf = core if mate == 0 else 1 - core
                below = dot_nn(high, at(table[2])[leaf, :S[2], :])
                below = (below + dot_nn(low, at(table[2])[leaf, S[2]:, :])).astype(bf)
                left, right = ((C, Z), (Cm, Zm))[mate]
                value = dot_nt(residual(3, mate, left, below), at(right[3])[...]).astype(bf)
                for r in range(R):
                    at(f3)[mate * R + r] = value[:, r * K[3]:(r + 1) * K[3]]
                leave(
                    3, lambda r: at(f3).at[mate * R + r], placed(3, z * N + core * NH),
                    c if mate == 0 else flipped(c, 1),
                )
        with phase(61):
            for l in levels:
                drain(0, l)
                if l:
                    drain(1, l)
                    arrived(at(Zm[l]), at(Zms[l]))
                    arrived(at(Cm[l]), at(Cms[l]))
                drain_rhs(l)
                if l < 3:
                    drain_spread(l)

            @pl.when(middle)
            def _():
                for l in lower:
                    arrived(at(y[l]).at[pl.ds(0, 3)], at(ys[l]))
                take(at(inner), sent[inner])
            take(at(plane), sent[plane])

            @pl.when(top_here)
            def _():
                arrived(at(xs0).at[pl.ds(0, R - 1)], at(Os[0]))

            @pl.when(jnp.logical_and(one_here, one_to == c))
            def _():
                arrived(at(f1).at[pl.ds(0, R - 1)], at(Os[1]))

            @pl.when(jnp.logical_and(one_here, one_to != c))
            def _():
                arrived(at(f1), at(Os[1]))

            @pl.when(two_to == c)
            def _():
                arrived(at(x2).at[:, pl.ds(0, S[2] - K[2])], at(Os[2]))

            @pl.when(two_to != c)
            def _():
                arrived(at(x2), at(Os[2]))
            arrived(at(f3).at[pl.ds(0, 2 * R - 1)], at(Os[3]))
        with phase(62):
            for l in levels:
                arrived(outs[l], at(Or[l]))

    return kernel, scratch


def hand_on(turned, *refs):
    for turn, source, target in zip(turned, refs[:4], refs[4:]):
        if turn:
            target[...] = dot_nt(eye(target.shape[0]), source[...]).astype(target.dtype)
        else:
            target[...] = source[...]


def fused_device(*blocks):
    plan = Plan(
        lax.axis_size("row"), lax.axis_size("col"),
        [block.shape for block in blocks[:4]], blocks[7].shape,
        [block.shape for block in blocks[11:14]],
    )
    if not plan.fits():
        return per_device(*blocks)
    kernel, scratch = build_kernel(plan)
    blocks = list(blocks)
    for at in (0, 1, 2, 3, 7, 8, 9, 10):
        if narrow(blocks[at].shape[1]):
            blocks[at] = blocks[at].T
    vmem = pl.BlockSpec(memory_space=pltpu.VMEM)
    anywhere = pl.BlockSpec(memory_space=pltpu.HBM)
    solved = pl.pallas_call(
        kernel,
        out_shape=tuple(
            jax.ShapeDtypeStruct((width, strip), blocks[0].dtype)
            for width, strip in zip(plan.width, plan.strip)
        ),
        in_specs=[anywhere] * 14,
        out_specs=(anywhere,) * 4,
        scratch_shapes=scratch,
        compiler_params=pltpu.CompilerParams(
            collective_id=0, has_side_effects=True, vmem_limit_bytes=VMEM_LIMIT
        ),
    )(*blocks)
    turned = [not narrow(width) for width in plan.width]
    solved = pl.pallas_call(
        functools.partial(hand_on, turned),
        out_shape=tuple(
            jax.ShapeDtypeStruct(block.shape[::-1] if turn else block.shape, block.dtype)
            for block, turn in zip(solved, turned)
        ),
        in_specs=[vmem] * 4,
        out_specs=(vmem,) * 4,
    )(*solved)
    return tuple(block if turn else block.T for block, turn in zip(solved, turned))


def solution(mesh):
    in_specs = (
        P("col", "row"),
        P("col", "row"),
        P("col", "row"),
        P("col", "row"),
        P("row", "col"),
        P("row", "col"),
        P("row", "col"),
        P("row", "col"),
        P("row", "col"),
        P("row", "col"),
        P("row", "col"),
        P(),
        P(),
        P(),
    )
    out_specs = (P("row", "col"), P("row", "col"), P("row", "col"), P("row", "col"))
    return jax.shard_map(
        fused_device, mesh=mesh, in_specs=in_specs, out_specs=out_specs, check_vma=False
    )
```

time: 75.7 us -> 59.3 us (0.78)
  Pallas kernels: 74.8 us -> 58.4 us
    pallas_call x2, Pallas kernels: 74.8 us -> 58.4 us  [the longest x1 56.7 us: fused_device(): pl.pallas_call(kernel, out_shape=tuple((jax.ShapeDtypeStruct((width, stri...]
where the time goes in v1:
time: 59.3 us; the launch traced here: 59.1 us
  Pallas kernels  58.4 us (98%)
  between operations  0.64 us (1%)
    pallas_call x1, Pallas kernels, fused_device(): pl.pallas_call(kernel, out_shape=tuple((jax.ShapeDtypeStruct((width, stri...  56.7 us
    pallas_call x1, Pallas kernels, fused_device(): pl.pallas_call(functools.partial(hand_on, turned), out_shape=tuple((jax.S...  1.7 us

profile of v1, /device:TPU:0, one launch (start us, length us, event | category | flops | bytes accessed | tf_op | source)
XLA Modules:
  0.0 59.1 jit_solution(2067376490044753296)
XLA Ops:
  0.6 56.7 %shard_map.165 = (bf16[32,256]{1,0:T(8,128)(2,1)}, bf16[64,192]{1,0:T(8,128)(2,1)}, bf16[128,128]{1,0:T(8,128)(2,1)}, bf16[256,64]{1,0:T(8,128)(2,1)}) custom-call(bf16[128,256]{1,0:T(8,128)(2,1)} %refs_0_.1, bf16[192,192]{1,0:T(8,128)(2,1)} %refs_1_.1, bf16[256,128]{1,0:T(8,128)(2,1)} %refs_2_.1, bf16[64,256]{1,0:T(8,128)(2,1)} %bitcast.5, ...), custom_call_target="tpu_custom_call" | custom-call | tf_op jit(solution)/shard_map/pallas_call | solution.py:1001
  57.4 1.7 %shard_map.166 = (bf16[32,256]{1,0:T(8,128)(2,1)}, bf16[64,192]{1,0:T(8,128)(2,1)}, bf16[128,128]{1,0:T(8,128)(2,1)}, bf16[64,256]{1,0:T(8,128)(2,1)}) custom-call(bf16[32,256]{1,0:T(8,128)(2,1)} %get-tuple-element.12.refs_0_, bf16[64,192]{1,0:T(8,128)(2,1)} %get-tuple-element.13.refs_1_, bf16[128,128]{1,0:T(8,128)(2,1)} %get-tuple-element.14.refs_2_, ...), custom_call_target="tpu_custom_call" | custom-call | tf_op jit(solution)/shard_map/pallas_call | solution.py:1015

commit v2 on v1

--- a/solution.py
+++ b/solution.py
@@ -214,7 +214,7 @@
 
 
 MESH = pl.DeviceIdType.MESH
-VMEM_LIMIT = 56 * 2**20
+VMEM_LIMIT = 32 * 2**20
 
 
 def dot_nn(left, right):
@@ -258,9 +258,9 @@
 
     def span_rows(self):
         n, order, width = self.mine, self.order, self.width
-        shared = 7 * (n // 4) * order[1] + 10 * (n // 2) * (order[0] // 4) + n // 2 * order[1]
-        inner = 2 * n * order[3] + 4 * n * order[2] + 7 * (n // 4) * order[1]
-        return max(shared, inner, 7 * width[0] * order[0], 3 * n * order[2]) // 128
+        shared = 3 * (n // 4) * order[1] + 3 * (n // 2) * order[0] + n // 2 * order[1]
+        inner = 2 * n * order[3] + 4 * n * order[2] + 8 * (n // 4) * order[1]
+        return max(shared, inner, 3 * width[0] * order[0], 3 * n * order[2]) // 128
 
     def fits(self):
         table = sum(
@@ -321,39 +321,40 @@
     c_shape = [None] + [(S[l], L[l]) for l in lower]
     Z = [ref(z_shape[l]) for l in levels]
     C = [None] + [ref(c_shape[l]) for l in lower]
-    Zm = [None] + [ref(z_shape[l]) for l in lower]
+    Zm = [ref(z_shape[l]) for l in levels]
     Cm = [None] + [ref(c_shape[l]) for l in lower]
     Zp = [ref((R,) + packed_shape((L[l], K[l]))) if l < 3 and packed((L[l], K[l])) else None for l in levels]
     Cp = [None] + [ref((R,) + packed_shape((K[l], L[l]))) if packed((K[l], L[l])) else None for l in lower]
     Zraw = [ref((L[l], K[l])) if Zp[l] is not None else None for l in levels]
     Craw = [None] + [ref((K[l], L[l])) if Cp[l] is not None else None for l in lower]
     Zr, Zs = [sems(R) for _ in levels], [sems() for _ in levels]
-    Cr, Cs = [sems(R) for _ in levels], [sems() for _ in levels]
+    Cr, Cs = [None] + [sems(R) for _ in lower], [None] + [sems() for _ in lower]
     Zmr, Zms = [sems() for _ in levels], [sems() for _ in levels]
-    Cmr, Cms = [sems() for _ in levels], [sems() for _ in levels]
+    Cmr, Cms = [None] + [sems() for _ in lower], [None] + [sems() for _ in lower]
     table = [ref((2, plan.total(l), S[l + 1])) for l in range(3)]
     held_map = [None] + [ref(plan.map_shape[l - 1], jnp.int32) for l in lower]
-    local = sems(8)
-    B = [ref((N, S[0])), ref((2, R) + packed_shape((N, K[1]))), ref((S[2], N2)), ref((S[3], N2))]
+    local = sems(6)
+    B = [ref((NH, S[0])), ref((2, R) + packed_shape((N, K[1]))), ref((S[2], N2)), ref((S[3], N2))]
     B1, rhs_raw, rhs_packed = ref((N2, S[1])), ref((N, K[1])), ref(packed_shape((N, K[1])))
     Bs, Br = [sems() for _ in levels], [sems() for _ in levels]
-    Ds, Dr = [sems(), sems(G[1]), sems()], [sems(2), sems(2), sems()]
-    y = [ref((N, L[0]))] + [ref((4, NH, L[l])) for l in lower]
+    Ds, Dr = [sems(), sems(G[1]), sems()], [sems(), sems(2), sems()]
+    y = [None] + [ref((4, NH, L[l])) for l in lower]
     yb = [None] + [ref((2, NH, L[l])) for l in lower]
-    ys, yr = [sems() for _ in levels], [sems() for _ in levels]
+    ys, yr = [None] + [sems() for _ in lower], [None] + [sems() for _ in lower]
     u = [None, ref((2, G[1], NQ, S[1])), ref((2, 2, G[1], NQ, S[2])), ref((2, N2, S[3]))]
-    ur = [sems() for _ in levels]
-    up1, ut1, ut1r = ref((2, G[1], NQ, S[1])), ref((G[1], NQ, S[1])), sems()
+    ur = [None] + [sems() for _ in lower]
+    up1, ut1, ut1r = ref((2, G[1], NQ, S[1])), ref((G[1] + 1, NQ, S[1])), sems()
     h1 = ref((2, NQ, S[1]))
+    folded, early1 = ref((2, L[1], S[2])), ref((N2, L[1]), jnp.float32)
     up2, ut2, ut2r = ref((2, N, S[2])), ref((N, S[2])), sems()
-    xp0, xr0, xr0r = ref((chips, 2, NH, S[0] // chips)), ref((CC, NH, S[0] // chips)), sems()
-    xs0, xs0r = ref((chips, NH, S[0] // chips)), sems()
+    xp0, xr0, xr0r = ref((NH, S[0])), ref((chips, NH, S[0])), sems()
+    x0 = ref((NH, S[0]))
     xp1, xr1, xr1r = ref((NH, S[1])), ref((NH, S[1])), sems()
     v = [None] + [ref((NH, S[l])) for l in (1, 2)]
     x1, x2 = ref((NH, S[1])), ref((NH, S[2]))
     f1, f3 = ref((R, NH, K[1])), ref((2 * R, NH, K[3]))
     Os, Or = [sems() for _ in levels], [sems() for _ in levels]
-    plane, inner = sems(), sems()
+    plane, inner, beside = sems(), sems(), sems()
     span = ref((plan.span_rows(), 128))
 
     def kernel(*refs):
@@ -403,13 +404,12 @@
         for friend in friends:
             pl.semaphore_signal(barrier, inc=1, device_id=friend, device_id_type=MESH)
 
-        raws = []
+        raws = [(rhs[1], at(rhs_raw))]
         for l in levels:
             if Zp[l] is not None:
                 raws.append((inverse[l], at(Zraw[l])))
             if l and Cp[l] is not None:
                 raws.append((coupling[l], at(Craw[l])))
-        raws.append((rhs[1], at(rhs_raw)))
         loads = raws + [(maps[l], at(held_map[l])) for l in lower]
         for i, (src, dst) in enumerate(loads):
             pltpu.make_async_copy(src, dst, at(local).at[i]).start()
@@ -524,9 +524,8 @@
                 return [(rhs[2], at(B[2]).at[pl.ds(pl.multiple_of(z * K[2], 16), K[2])], 1 + q)]
             if l == 1:
                 return [(at(rhs_packed), at(B[1]).at[q % 2, z], 1 + q // 2)]
-            rows = pl.ds(pl.multiple_of((q % 2) * W[0], W[0]), W[0])
             lanes = pl.ds(pl.multiple_of(z * K[0], 128), K[0])
-            return [(rhs[0], at(B[0]).at[rows, lanes], q // 2)]
+            return [(rhs[0], at(B[0]).at[:, lanes], q // 2)]
 
         def start_rhs(l):
             for src, dst, z_to in rhs_pieces(l):
@@ -561,8 +560,7 @@
                 return z == 1 + q, at(B[2]), at(Dr[2])
             if l == 1:
                 return z == 1 + q // 2, at(B[1]).at[q % 2], at(Dr[1]).at[q % 2]
-            rows = pl.ds(pl.multiple_of((q % 2) * W[0], W[0]), W[0])
-            return z == q // 2, at(B[0]).at[rows], at(Dr[0]).at[q % 2]
+            return z == q // 2, at(B[0]), at(Dr[0])
 
         def spread_rhs(l):
             holds, here, rsem = rhs_spread(l)
@@ -570,7 +568,7 @@
             @pl.when(holds)
             def _():
                 arrived(here, at(Br[l]))
-                for m in range(1, G[l]):
+                for m in range(2, CC, 2) if l == 0 else range(1, G[l]):
                     ssem = at(Ds[l]).at[m] if l == 1 else at(Ds[l])
                     push(here, here, ssem, rsem, z, flipped(c, m))
 
@@ -583,11 +581,11 @@
                     for m in range(1, G[l]):
                         arrived(here, at(Ds[l]).at[m])
                 else:
-                    take(at(Ds[l]), (G[l] - 1) * elements(here.shape))
+                    take(at(Ds[l]), (1 if l else chips - 1) * elements(here.shape))
 
         def wait_rhs(l):
             holds, here, rsem = rhs_spread(l)
-            if l == 2:
+            if l != 1:
                 @pl.when(jnp.logical_not(holds))
                 def _():
                     arrived(here, rsem)
@@ -595,8 +593,7 @@
             for part in range(2):
                 @pl.when(jnp.logical_not(jnp.logical_and(holds, c % 2 == part)))
                 def _():
-                    view = at(B[1]).at[part] if l == 1 else at(B[0]).at[pl.ds(part * W[0], W[0])]
-                    arrived(view, at(Dr[l]).at[part])
+                    arrived(at(B[1]).at[part], at(Dr[1]).at[part])
 
         def make_table(l):
             front = c // G[l]
@@ -624,28 +621,29 @@
                 own, copy, at((Zms, Cms)[kind][l]), at((Zmr, Cmr)[kind][l]), z, flipped(c, 1)
             )
 
-        with phase(1):
-            for i, (src, dst) in enumerate(loads):
-                pltpu.make_async_copy(src, dst, at(local).at[i]).wait()
+        with phase(2):
+            pl.semaphore_wait(barrier, len(friends))
+
+        with phase(3):
+            own_send(0, 3)
+            start_rhs(3)
+            own_send(1, 3)
+            pltpu.make_async_copy(*loads[0], at(local).at[0]).wait()
+            at(rhs_packed)[...] = pack(at(rhs_raw))
+            start_rhs(2)
+            start_rhs(1)
+            own_send(0, 2)
+            own_send(1, 2)
+            for i, (src, dst) in enumerate(loads[1:]):
+                pltpu.make_async_copy(src, dst, at(local).at[i + 1]).wait()
             for l in levels:
                 if Zp[l] is not None:
                     at(Zp[l])[z] = pack(at(Zraw[l]))
                 if l and Cp[l] is not None:
                     at(Cp[l])[z] = pack(at(Craw[l]))
-            at(rhs_packed)[...] = pack(at(rhs_raw))
-        with phase(2):
-            pl.semaphore_wait(barrier, len(friends))
-
-        with phase(3):
-            own_send(0, 3)
-            start_rhs(3)
-            own_send(1, 3)
-            for l in (2, 1, 0):
-                start_rhs(l)
-            own_send(0, 2)
-            own_send(1, 2)
             own_send(0, 1)
             own_send(1, 1)
+            start_rhs(0)
             own_send(0, 0)
             for l in levels:
                 own_load(0, l)
@@ -676,8 +674,8 @@
                 counted(here, here, inner, at(ur[3]), z, flipped(c, 1))
                 pass_on(0, 3)
                 pass_on(1, 3)
-        for l in (2, 1, 0):
-            spread_rhs(l)
+        spread_rhs(2)
+        spread_rhs(1)
         make_table(1)
 
         @pl.when(middle)
@@ -724,34 +722,42 @@
                     for r in range(R):
                         value = unpacked(at(B[1])[part, r], N, K[1])
                         at(B1)[part * N:(part + 1) * N, r * K[1]:(r + 1) * K[1]] = value
+            with phase(14):
+                settle_all(0, 1)
+            with phase(10):
+                at(early1)[...] = dot_nt(at(B1)[...], at(Z[1])[...])
+                for i in range(2):
+                    at(folded)[i] = dot_nn(at(Z[1])[...], at(table[1])[i, :S[1], :]).astype(bf)
             with phase(12):
                 take(at(ur[2]), 3 * N * S[2])
             with phase(13):
                 pair_of = [at(u[2])[i].reshape(N2, S[2]) for i in range(2)]
-                right = at(B1)[...].astype(jnp.float32) + gathered(1, 0, S[1], *pair_of)
-                right = right.astype(bf)
-                pair_of = [at(u[2])[i, :, q].reshape(2 * NQ, S[2]) for i in range(2)]
-                kept = gathered(1, S[1], S[1], *pair_of)
-                at(h1)[...] = kept.astype(bf).reshape(2, NQ, S[1])
-            with phase(14):
-                settle_all(0, 1)
-            with phase(15):
-                solved = dot_nt(right, at(Z[1])[...]).astype(bf)
+                solved = at(early1)[...]
+                for i in range(2):
+                    solved = solved + dot_nt(pair_of[i], at(folded)[i])
+                solved = solved.astype(bf)
                 at(y[1])[...] = solved.reshape(4, NH, L[1])
             with phase(16):
                 settle_all(1, 1)
             with phase(17):
                 coupled = dot_nt(solved, at(C[1])[...])
                 at(up1)[...] = coupled.astype(bf).reshape(2, G[1], NQ, S[1])
-                at(up1)[1 - half, q] = (
-                    at(up1)[1 - half, q].astype(jnp.float32) - at(h1)[1 - half].astype(jnp.float32)
-                ).astype(bf)
                 for m in range(G[1]):
                     src = at(up1).at[1 - half, flipped(q, m)]
                     counted(src, at(ut1).at[m], inner, at(ut1r), pair, flipped(c, m))
                 for m in range(1, G[1]):
                     src = at(up1).at[half, flipped(q, m)]
                     counted(src, at(ut1).at[m], inner, at(ut1r), z, flipped(c, m))
+                pair_of = [at(u[2])[i, :, q].reshape(2 * NQ, S[2]) for i in range(2)]
+                kept = gathered(1, S[1], S[1], *pair_of)
+                at(h1)[...] = kept.astype(bf).reshape(2, NQ, S[1])
+                counted(at(h1).at[1 - half], at(ut1).at[G[1]], inner, at(ut1r), pair, c)
+                spread_rhs(0)
+                settle(0, 0, (z, pair, across, beyond))
+                pass_on(0, 0)
+                pass_on(0, 1)
+                pass_on(1, 1)
+                forward(0, 0)
 
         @pl.when(border)
         def _():
@@ -760,11 +766,12 @@
                     for kind in range(2):
                         settle_all(kind, l)
                         forward(kind, l)
+                spread_rhs(0)
                 arrived(at(ut1), at(ut1r))
                 value = at(ut1)[0].astype(jnp.float32)
                 for m in range(1, G[1]):
                     value = value + at(ut1)[m].astype(jnp.float32)
-                at(u[1])[child, q] = (-value).astype(bf)
+                at(u[1])[child, q] = (at(ut1)[G[1]].astype(jnp.float32) - value).astype(bf)
 
         @pl.when(middle)
         def _():
@@ -775,8 +782,19 @@
                     value = value + at(ut1)[m].astype(jnp.float32)
                 at(u[1])[child, q] = (at(h1)[half].astype(jnp.float32) - value).astype(bf)
         here = at(u[1]).at[child, q]
-        for m in range(1, CC):
-            counted(here, here, plane, at(ur[1]), z, flipped(c, m))
+        kept_here = q // 2 == core
+        for m in range(2, CC, 2):
+            counted(here, here, plane, at(ur[1]), z, flipped(2 * chip + q // 2, m))
+
+        @pl.when(jnp.logical_not(kept_here))
+        def _():
+            push(here, here, at(beside), at(ur[1]), z, flipped(c, 1))
+
+        @pl.when(border)
+        def _():
+            with phase(40):
+                settle(0, 0, (z, pair, across, beyond))
+                forward(0, 0)
 
         @pl.when(middle)
         def _():
@@ -792,50 +810,51 @@
                 for l in lower:
                     for kind in range(2):
                         forward(kind, l)
-                settle(0, 0, (across, beyond))
-                pass_on(0, 0)
-                pass_on(0, 1)
-                pass_on(1, 1)
         with phase(41):
-            take(at(ur[1]), (CC - 1) * NQ * S[1])
+            @pl.when(kept_here)
+            def _():
+                take(at(ur[1]), 3 * NQ * S[1])
+
+            @pl.when(jnp.logical_not(kept_here))
+            def _():
+                take(at(ur[1]), 4 * NQ * S[1])
             wait_rhs(0)
         with phase(42):
-            pair_of = [at(u[1])[i].reshape(N, S[1]) for i in range(2)]
+            columns = pl.ds(pl.multiple_of(2 * core, 2), 2)
+            pair_of = [at(u[1])[i, columns].reshape(NH, S[1]) for i in range(2)]
             right = at(B[0])[...].astype(jnp.float32) + gathered(0, 0, S[0], *pair_of)
             right = right.astype(bf)
         with phase(43):
-            settle(0, 0, (z, pair))
-
-            @pl.when(border)
-            def _():
-                settle(0, 0, (across, beyond))
+            arrived(at(Zm[0]), at(Zmr[0]))
         with phase(44):
-            solved = dot_nt(right, at(Z[0])[...]).astype(bf)
-            value = dot_nn(solved, at(Z[0])[...]).astype(bf)
-            wide = S[0] // chips
-            for j in range(chips):
-                at(xp0)[j] = value[:, j * wide:(j + 1) * wide].reshape(2, NH, wide)
-            for m in range(1, CC):
-                to = flipped(c, m)
-                counted(at(xp0).at[to // 2, to % 2], at(xr0).at[m], plane, at(xr0r), z, to)
+            value = 0.0
+            for blocks in (Z, Zm):
+                solved = dot_nt(right, at(blocks[0])[...]).astype(bf)
+                value = value + dot_nn(solved, at(blocks[0])[...])
+            value = value.astype(bf)
+            at(xp0)[...] = value
+            for m in (3, 1, 2):
+                counted(at(xp0), at(xr0).at[m], plane, at(xr0r), z, flipped(c, 2 * m))
 
         @pl.when(border)
         def _():
             with phase(45):
-                for kind in range(2):
-                    settle_all(kind, 1)
-                    forward(kind, 1)
+                settle_all(0, 1)
+                forward(0, 1)
+
+        @pl.when(border)
+        def _():
+            with phase(48):
+                settle_all(1, 1)
+                forward(1, 1)
         with phase(46):
-            value = at(xp0)[chip, core].astype(jnp.float32)
-            arrived(at(xr0).at[pl.ds(1, CC - 1)], at(xr0r))
-            for m in range(1, CC):
+            arrived(at(xr0).at[pl.ds(1, chips - 1)], at(xr0r))
+        with phase(47):
+            value = at(xp0)[...].astype(jnp.float32)
+            for m in range(1, chips):
                 value = value + at(xr0)[m].astype(jnp.float32)
-            at(xs0)[chip] = value.astype(bf)
-            here = at(xs0).at[chip]
-            for m in range(2, CC, 2):
-                counted(here, here, plane, at(xs0r), z, flipped(c, m))
-        with phase(47):
-            arrived(at(xs0).at[pl.ds(1, chips - 1)], at(xs0r))
+            value = value.astype(bf)
+            at(x0)[...] = value
 
         def leave(l, piece, dst, c_to):
             @pl.when(c_to == c)
@@ -852,19 +871,18 @@
         top_here, one_here = chip == z, q // 2 == z // 2
         one_to, two_to = 2 * chip + z % 2, 2 * chip + z // 2
 
+        def top_piece(r):
+            return at(x0).at[:, pl.ds(pl.multiple_of(r * K[0], 128), K[0])]
+
         @pl.when(top_here)
         def _():
-            leave(0, lambda r: at(xs0).at[r], outs[0], c)
+            leave(0, top_piece, outs[0], c)
 
         def placed(l, low):
             return outs[l].at[pl.ds(pl.multiple_of(low, 16), NH)]
 
         with phase(51):
-            value = None
-            for r in range(chips):
-                part = dot_nn(at(xs0)[r], at(table[0])[child, r * wide:(r + 1) * wide, :])
-                value = part if value is None else value + part
-            at(v[1])[...] = value.astype(bf)
+            at(v[1])[...] = dot_nn(value, at(table[0])[child]).astype(bf)
             low = at(v[1])[...]
 
         def residual(l, index, coupled, low):
@@ -933,9 +951,9 @@
         with phase(61):
             for l in levels:
                 drain(0, l)
+                arrived(at(Zm[l]), at(Zms[l]))
                 if l:
                     drain(1, l)
-                    arrived(at(Zm[l]), at(Zms[l]))
                     arrived(at(Cm[l]), at(Cms[l]))
                 drain_rhs(l)
                 if l < 3:
@@ -948,9 +966,13 @@
                 take(at(inner), sent[inner])
             take(at(plane), sent[plane])
 
+            @pl.when(jnp.logical_not(kept_here))
+            def _():
+                arrived(at(u[1]).at[child, q], at(beside))
+
             @pl.when(top_here)
             def _():
-                arrived(at(xs0).at[pl.ds(0, R - 1)], at(Os[0]))
+                arrived(at(x0).at[:, pl.ds(0, S[0] - K[0])], at(Os[0]))
 
             @pl.when(jnp.logical_and(one_here, one_to == c))
             def _():
@@ -976,7 +998,11 @@
 
 
 def hand_on(turned, *refs):
-    for turn, source, target in zip(turned, refs[:4], refs[4:]):
+    arriving = refs[12]
+    for i in range(4):
+        pltpu.make_async_copy(refs[i], refs[8 + i], arriving.at[i]).start()
+    for i, (turn, source, target) in enumerate(zip(turned, refs[8:12], refs[4:8])):
+        pltpu.make_async_copy(refs[i], source, arriving.at[i]).wait()
         if turn:
             target[...] = dot_nt(eye(target.shape[0]), source[...]).astype(target.dtype)
         else:
@@ -996,6 +1022,7 @@
     for at in (0, 1, 2, 3, 7, 8, 9, 10):
         if narrow(blocks[at].shape[1]):
             blocks[at] = blocks[at].T
+    blocks = [pltpu.with_memory_space_constraint(block, pltpu.HBM) for block in blocks]
     vmem = pl.BlockSpec(memory_space=pltpu.VMEM)
     anywhere = pl.BlockSpec(memory_space=pltpu.HBM)
     solved = pl.pallas_call(
@@ -1005,7 +1032,7 @@
             for width, strip in zip(plan.width, plan.strip)
         ),
         in_specs=[anywhere] * 14,
-        out_specs=(anywhere,) * 4,
+        out_specs=(pl.BlockSpec(memory_space=pl.ANY),) * 4,
         scratch_shapes=scratch,
         compiler_params=pltpu.CompilerParams(
             collective_id=0, has_side_effects=True, vmem_limit_bytes=VMEM_LIMIT
@@ -1018,8 +1045,11 @@
             jax.ShapeDtypeStruct(block.shape[::-1] if turn else block.shape, block.dtype)
             for block, turn in zip(solved, turned)
         ),
-        in_specs=[vmem] * 4,
+        in_specs=[pl.BlockSpec(memory_space=pl.ANY)] * 4,
         out_specs=(vmem,) * 4,
+        scratch_shapes=[pltpu.VMEM(block.shape, block.dtype) for block in solved]
+        + [pltpu.SemaphoreType.DMA((4,))],
+        compiler_params=pltpu.CompilerParams(vmem_limit_bytes=2**20),
     )(*solved)
     return tuple(block if turn else block.T for block, turn in zip(solved, turned))
 

time: 59.3 us -> 52.9 us (0.89)
  Pallas kernels: 58.4 us -> 52.1 us
    pallas_call x1, Pallas kernels: 56.7 us -> 50.9 us  [fused_device(): pl.pallas_call(kernel, out_shape=tuple((jax.ShapeDtypeStruct((width, stri...]
where the time goes in v2:
time: 52.9 us; the launch traced here: 52.8 us
  Pallas kernels  52.1 us (98%)
  between operations  0.64 us (1%)
    pallas_call x1, Pallas kernels, fused_device(): pl.pallas_call(kernel, out_shape=tuple((jax.ShapeDtypeStruct((width, stri...  50.9 us
    pallas_call x1, Pallas kernels, fused_device(): pl.pallas_call(functools.partial(hand_on, turned), out_shape=tuple((jax.S...  1.18 us

profile of v2, /device:TPU:0, one launch (start us, length us, event | category | flops | bytes accessed | tf_op | source)
XLA Modules:
  0.0 52.8 jit_solution(16390941866621373237)
XLA Ops:
  0.6 50.9 %shard_map.165 = (bf16[32,256]{1,0:T(8,128)(2,1)S(1)}, bf16[64,192]{1,0:T(8,128)(2,1)S(1)}, bf16[128,128]{1,0:T(8,128)(2,1)S(1)}, bf16[256,64]{1,0:T(8,128)(2,1)S(1)}) custom-call(bf16[128,256]{1,0:T(8,128)(2,1)} %refs_0_.1, bf16[192,192]{1,0:T(8,128)(2,1)} %refs_1_.1, bf16[256,128]{1,0:T(8,128)(2,1)} %refs_2_.1, bf16[64,256]{1,0:T(8,128)(2,1)} %bitcast.5, ...), custom_call_target="tpu_custom_call" | custom-call | tf_op jit(solution)/shard_map/pallas_call | solution.py:1028
  51.6 1.2 %shard_map.166 = (bf16[32,256]{1,0:T(8,128)(2,1)}, bf16[64,192]{1,0:T(8,128)(2,1)}, bf16[128,128]{1,0:T(8,128)(2,1)}, bf16[64,256]{1,0:T(8,128)(2,1)}) custom-call(bf16[32,256]{1,0:T(8,128)(2,1)S(1)} %get-tuple-element.12.refs_0_, bf16[64,192]{1,0:T(8,128)(2,1)S(1)} %get-tuple-element.13.refs_1_, bf16[128,128]{1,0:T(8,128)(2,1)S(1)} %get-tuple-element.14.refs_2_, ...), custom_call_target="tpu_custom_call" | custom-call | tf_op jit(solution)/shard_map/pallas_call | solution.py:1042

commit v3 on v2

--- a/solution.py
+++ b/solution.py
@@ -256,11 +256,17 @@
     def total(self, level):
         return self.order[level] * (2 if level else 1)
 
+    def result_shapes(self):
+        shapes = list(zip(self.width, self.strip))
+        return shapes[:3] + [(self.width[3] // 2, 2 * self.strip[3])]
+
     def span_rows(self):
         n, order, width = self.mine, self.order, self.width
         shared = 3 * (n // 4) * order[1] + 3 * (n // 2) * order[0] + n // 2 * order[1]
         inner = 2 * n * order[3] + 4 * n * order[2] + 8 * (n // 4) * order[1]
-        return max(shared, inner, 3 * width[0] * order[0], 3 * n * order[2]) // 128
+        joined = sum(2 * order[level] * self.local[level] for level in (2, 3))
+        joined += sum(order[level] * self.local[level] for level in (0, 1))
+        return max(shared, inner, joined, 9 * n * order[1], 3 * width[0] * order[0], 3 * n * order[2]) // 128
 
     def fits(self):
         table = sum(
@@ -327,23 +333,23 @@
     Cp = [None] + [ref((R,) + packed_shape((K[l], L[l]))) if packed((K[l], L[l])) else None for l in lower]
     Zraw = [ref((L[l], K[l])) if Zp[l] is not None else None for l in levels]
     Craw = [None] + [ref((K[l], L[l])) if Cp[l] is not None else None for l in lower]
-    Zr, Zs = [sems(R) for _ in levels], [sems() for _ in levels]
-    Cr, Cs = [None] + [sems(R) for _ in lower], [None] + [sems() for _ in lower]
-    Zmr, Zms = [sems() for _ in levels], [sems() for _ in levels]
-    Cmr, Cms = [None] + [sems() for _ in lower], [None] + [sems() for _ in lower]
+    Zr, Zs = [sems() for _ in levels], [sems() for _ in levels]
+    Cr, Cs = [None] + [sems() for _ in lower], [None] + [sems() for _ in lower]
+    Zmr, Cmr, mates, mates1 = [sems() for _ in levels], [None] + [sems() for _ in lower], sems(), sems()
     table = [ref((2, plan.total(l), S[l + 1])) for l in range(3)]
     held_map = [None] + [ref(plan.map_shape[l - 1], jnp.int32) for l in lower]
     local = sems(6)
     B = [ref((NH, S[0])), ref((2, R) + packed_shape((N, K[1]))), ref((S[2], N2)), ref((S[3], N2))]
     B1, rhs_raw, rhs_packed = ref((N2, S[1])), ref((N, K[1])), ref(packed_shape((N, K[1])))
     Bs, Br = [sems() for _ in levels], [sems() for _ in levels]
-    Ds, Dr = [sems(), sems(G[1]), sems()], [sems(), sems(2), sems()]
+    Ds, Dr = [sems(), sems(), sems()], [sems(), sems(2), sems()]
     y = [None] + [ref((4, NH, L[l])) for l in lower]
     yb = [None] + [ref((2, NH, L[l])) for l in lower]
     ys, yr = [None] + [sems() for _ in lower], [None] + [sems() for _ in lower]
     u = [None, ref((2, G[1], NQ, S[1])), ref((2, 2, G[1], NQ, S[2])), ref((2, N2, S[3]))]
-    ur = [None] + [sems() for _ in lower]
-    up1, ut1, ut1r = ref((2, G[1], NQ, S[1])), ref((G[1] + 1, NQ, S[1])), sems()
+    ur, ur1 = [None, None, sems(), sems()], sems(2)
+    f0 = ref((NH, S[0]), jnp.float32)
+    up1, ut1, ut1r = ref((2, G[1], NQ, S[1])), ref((G[1], NQ, S[1])), sems()
     h1 = ref((2, NQ, S[1]))
     folded, early1 = ref((2, L[1], S[2])), ref((N2, L[1]), jnp.float32)
     up2, ut2, ut2r = ref((2, N, S[2])), ref((N, S[2])), sems()
@@ -352,9 +358,12 @@
     xp1, xr1, xr1r = ref((NH, S[1])), ref((NH, S[1])), sems()
     v = [None] + [ref((NH, S[l])) for l in (1, 2)]
     x1, x2 = ref((NH, S[1])), ref((NH, S[2]))
-    f1, f3 = ref((R, NH, K[1])), ref((2 * R, NH, K[3]))
+    f1, f3 = ref((R, NH, K[1])), ref((2 * R, NH // 2, 2 * K[3]))
+    folded3 = ref((2, 2 * S[2], L[3]))
     Os, Or = [sems() for _ in levels], [sems() for _ in levels]
     plane, inner, beside = sems(), sems(), sems()
+    scratch.append(pltpu.SemaphoreType.REGULAR)
+    ready = len(scratch) - 1
     span = ref((plan.span_rows(), 128))
 
     def kernel(*refs):
@@ -397,12 +406,17 @@
             pltpu.make_async_copy(view, view, sem).wait()
 
         barrier = pltpu.get_barrier_semaphore()
-        friends = [(z, flipped(c, m)) for m in range(1, CC)]
-        for d in range(1, R):
-            friends += [((z + d) % R, c), ((z + d) % R, flipped(c, 1))]
-        friends += [(pair, flipped(c, m)) for m in range(2, G[1])]
-        for friend in friends:
-            pl.semaphore_signal(barrier, inc=1, device_id=friend, device_id_type=MESH)
+        mates_here = [(z, flipped(c, m)) for m in range(1, CC)]
+
+        def greet(semaphore, *friends):
+            for friend in friends:
+                pl.semaphore_signal(semaphore, inc=1, device_id=friend, device_id_type=MESH)
+
+        greet(barrier, (pair, c))
+
+        @pl.when(middle)
+        def _():
+            greet(barrier, (across, c), (beyond, c), *mates_here)
 
         raws = [(rhs[1], at(rhs_raw))]
         for l in levels:
@@ -417,16 +431,16 @@
         def slot(kind, l, r):
             if kind == 0:
                 if Zp[l] is not None:
-                    return at(Zp[l]).at[r], at(Zr[l]).at[r]
+                    return at(Zp[l]).at[r], at(Zr[l])
                 if l == 3:
                     low = pl.multiple_of(r * K[l], 16)
-                    return at(Z[l]).at[pl.ds(low, K[l])], at(Zr[l]).at[r]
+                    return at(Z[l]).at[pl.ds(low, K[l])], at(Zr[l])
                 low = pl.multiple_of(r * K[l], 128)
-                return at(Z[l]).at[:, pl.ds(low, K[l])], at(Zr[l]).at[r]
+                return at(Z[l]).at[:, pl.ds(low, K[l])], at(Zr[l])
             if Cp[l] is not None:
-                return at(Cp[l]).at[r], at(Cr[l]).at[r]
+                return at(Cp[l]).at[r], at(Cr[l])
             low = pl.multiple_of(r * K[l], 16)
-            return at(C[l]).at[pl.ds(low, K[l])], at(Cr[l]).at[r]
+            return at(C[l]).at[pl.ds(low, K[l])], at(Cr[l])
 
         def is_packed(kind, l):
             return (Zp, Cp)[kind][l] is not None
@@ -456,19 +470,18 @@
             dst, sem = slot(kind, l, z)
             push(source(kind, l), dst, send_sem(kind, l), sem, pair, c)
 
-        def pass_on(kind, l):
-            for r in (across, beyond):
+        def pass_on(kind, l, origins=(across, beyond)):
+            for r in origins:
                 dst, sem = slot(kind, l, r)
                 push(dst, dst, send_sem(kind, l), sem, pair, c)
 
-        def settle(kind, l, which):
-            for r in which:
-                arrived(*slot(kind, l, r))
-
         def settle_all(kind, l):
-            settle(kind, l, (pair, across, beyond) if is_packed(kind, l) else (z, pair, across, beyond))
+            rsem = slot(kind, l, z)[1]
             if is_packed(kind, l):
+                arrived(at((Zp, Cp)[kind][l]).at[pl.ds(0, R - 1)], rsem)
                 unpack(kind, l)
+            else:
+                arrived(at((Z, C)[kind][l]), rsem)
 
         def unpacked(block, rows, lanes):
             whole = lanes // 128 * rows
@@ -569,19 +582,14 @@
             def _():
                 arrived(here, at(Br[l]))
                 for m in range(2, CC, 2) if l == 0 else range(1, G[l]):
-                    ssem = at(Ds[l]).at[m] if l == 1 else at(Ds[l])
-                    push(here, here, ssem, rsem, z, flipped(c, m))
+                    push(here, here, at(Ds[l]), rsem, z, flipped(c, m))
 
         def drain_spread(l):
             holds, here, _ = rhs_spread(l)
 
             @pl.when(holds)
             def _():
-                if l == 1:
-                    for m in range(1, G[l]):
-                        arrived(here, at(Ds[l]).at[m])
-                else:
-                    take(at(Ds[l]), (1 if l else chips - 1) * elements(here.shape))
+                take(at(Ds[l]), (chips - 1, G[1] - 1, 1)[l] * elements(here.shape))
 
         def wait_rhs(l):
             holds, here, rsem = rhs_spread(l)
@@ -617,12 +625,26 @@
 
         def forward(kind, l):
             own, copy = at((Z, C)[kind][l]), at((Zm, Cm)[kind][l])
-            push(
-                own, copy, at((Zms, Cms)[kind][l]), at((Zmr, Cmr)[kind][l]), z, flipped(c, 1)
-            )
+            ssem = at(mates1 if own.shape[1] % 128 else mates)
+            push(own, copy, ssem, at((Zmr, Cmr)[kind][l]), z, flipped(c, 1))
+
+        def hand_over(l):
+            at(yb[l])[0] = at(y[l])[2 * half + core]
+            src = at(y[l]).at[2 * half + 1 - core]
+            push(src, at(yb[l]).at[1], at(ys[l]), at(yr[l]), z, flipped(c, 1))
+            src = at(y[l]).at[2 * (1 - half) + core]
+            push(src, at(yb[l]).at[0], at(ys[l]), at(yr[l]), pair, c)
+            src = at(y[l]).at[2 * (1 - half) + 1 - core]
+            push(src, at(yb[l]).at[1], at(ys[l]), at(yr[l]), pair, flipped(c, 1))
 
         with phase(2):
-            pl.semaphore_wait(barrier, len(friends))
+            @pl.when(middle)
+            def _():
+                pl.semaphore_wait(barrier, CC + 1)
+
+            @pl.when(border)
+            def _():
+                pl.semaphore_wait(barrier, 2)
 
         with phase(3):
             own_send(0, 3)
@@ -643,8 +665,6 @@
                     at(Cp[l])[z] = pack(at(Craw[l]))
             own_send(0, 1)
             own_send(1, 1)
-            start_rhs(0)
-            own_send(0, 0)
             for l in levels:
                 own_load(0, l)
                 if l:
@@ -656,6 +676,7 @@
                 for l in (3, 2, 1):
                     own_out(0, l)
                     own_out(1, l)
+                greet(at(ready), *mates_here)
         make_table(2)
 
         @pl.when(middle)
@@ -664,6 +685,10 @@
                 arrived(at(B[3]), at(Br[3]))
                 right = dot_nt(eye(N2), at(B[3])[...]).astype(bf)
                 settle_all(0, 3)
+                start_rhs(0)
+                own_send(0, 0)
+                pl.semaphore_wait(at(ready), CC - 1)
+                greet(at(ready), (pair, c))
             with phase(32):
                 solved = dot_nn(right, at(Z[3])[...]).astype(bf)
                 at(y[3])[...] = solved.reshape(4, NH, L[3])
@@ -698,7 +723,6 @@
                 at(y[2])[...] = solved.reshape(4, NH, L[2])
             with phase(25):
                 settle_all(1, 2)
-                pass_on(1, 2)
             with phase(26):
                 at(up2)[...] = dot_nt(solved, at(C[2])[...]).astype(bf).reshape(2, N, S[2])
                 counted(at(up2).at[1 - core], at(ut2), inner, at(ut2r), z, flipped(c, 1))
@@ -724,6 +748,7 @@
                         at(B1)[part * N:(part + 1) * N, r * K[1]:(r + 1) * K[1]] = value
             with phase(14):
                 settle_all(0, 1)
+                pass_on(0, 1)
             with phase(10):
                 at(early1)[...] = dot_nt(at(B1)[...], at(Z[1])[...])
                 for i in range(2):
@@ -742,7 +767,7 @@
             with phase(17):
                 coupled = dot_nt(solved, at(C[1])[...])
                 at(up1)[...] = coupled.astype(bf).reshape(2, G[1], NQ, S[1])
-                for m in range(G[1]):
+                for m in range(1, G[1]):
                     src = at(up1).at[1 - half, flipped(q, m)]
                     counted(src, at(ut1).at[m], inner, at(ut1r), pair, flipped(c, m))
                 for m in range(1, G[1]):
@@ -751,27 +776,36 @@
                 pair_of = [at(u[2])[i, :, q].reshape(2 * NQ, S[2]) for i in range(2)]
                 kept = gathered(1, S[1], S[1], *pair_of)
                 at(h1)[...] = kept.astype(bf).reshape(2, NQ, S[1])
-                counted(at(h1).at[1 - half], at(ut1).at[G[1]], inner, at(ut1r), pair, c)
+                at(up1)[1 - half, q] = (
+                    at(up1)[1 - half, q].astype(jnp.float32) - at(h1)[1 - half].astype(jnp.float32)
+                ).astype(bf)
+                counted(at(up1).at[1 - half, q], at(ut1).at[0], inner, at(ut1r), pair, c)
                 spread_rhs(0)
-                settle(0, 0, (z, pair, across, beyond))
+                settle_all(0, 0)
                 pass_on(0, 0)
-                pass_on(0, 1)
                 pass_on(1, 1)
+                hand_over(1)
+                pass_on(1, 2)
+                hand_over(2)
+                hand_over(3)
                 forward(0, 0)
 
         @pl.when(border)
         def _():
             with phase(18):
-                for l in (3, 2):
-                    for kind in range(2):
-                        settle_all(kind, l)
-                        forward(kind, l)
+                pl.semaphore_wait(at(ready), 1)
+                for kind, l in ((0, 3), (1, 3), (0, 2)):
+                    settle_all(kind, l)
+                    if (kind, l) == (0, 3):
+                        start_rhs(0)
+                        own_send(0, 0)
+                    forward(kind, l)
                 spread_rhs(0)
                 arrived(at(ut1), at(ut1r))
                 value = at(ut1)[0].astype(jnp.float32)
                 for m in range(1, G[1]):
                     value = value + at(ut1)[m].astype(jnp.float32)
-                at(u[1])[child, q] = (at(ut1)[G[1]].astype(jnp.float32) - value).astype(bf)
+                at(u[1])[child, q] = (-value).astype(bf)
 
         @pl.when(middle)
         def _():
@@ -784,46 +818,42 @@
         here = at(u[1]).at[child, q]
         kept_here = q // 2 == core
         for m in range(2, CC, 2):
-            counted(here, here, plane, at(ur[1]), z, flipped(2 * chip + q // 2, m))
+            rsem = at(ur1).at[0 if m == 2 else 1]
+            counted(here, here, plane, rsem, z, flipped(2 * chip + q // 2, m))
 
         @pl.when(jnp.logical_not(kept_here))
         def _():
-            push(here, here, at(beside), at(ur[1]), z, flipped(c, 1))
+            push(here, here, at(beside), at(ur1).at[0], z, flipped(c, 1))
 
         @pl.when(border)
         def _():
             with phase(40):
-                settle(0, 0, (z, pair, across, beyond))
+                settle_all(0, 0)
                 forward(0, 0)
 
         @pl.when(middle)
         def _():
             with phase(20):
-                for l in lower:
-                    at(yb[l])[0] = at(y[l])[2 * half + core]
-                    src = at(y[l]).at[2 * half + 1 - core]
-                    push(src, at(yb[l]).at[1], at(ys[l]), at(yr[l]), z, flipped(c, 1))
-                    src = at(y[l]).at[2 * (1 - half) + core]
-                    push(src, at(yb[l]).at[0], at(ys[l]), at(yr[l]), pair, c)
-                    src = at(y[l]).at[2 * (1 - half) + 1 - core]
-                    push(src, at(yb[l]).at[1], at(ys[l]), at(yr[l]), pair, flipped(c, 1))
                 for l in lower:
                     for kind in range(2):
                         forward(kind, l)
         with phase(41):
             @pl.when(kept_here)
             def _():
-                take(at(ur[1]), 3 * NQ * S[1])
+                take(at(ur1).at[0], NQ * S[1])
 
             @pl.when(jnp.logical_not(kept_here))
             def _():
-                take(at(ur[1]), 4 * NQ * S[1])
+                take(at(ur1).at[0], 2 * NQ * S[1])
             wait_rhs(0)
+        columns = pl.ds(pl.multiple_of(2 * core, 2), 2)
         with phase(42):
-            columns = pl.ds(pl.multiple_of(2 * core, 2), 2)
-            pair_of = [at(u[1])[i, columns].reshape(NH, S[1]) for i in range(2)]
-            right = at(B[0])[...].astype(jnp.float32) + gathered(0, 0, S[0], *pair_of)
-            right = right.astype(bf)
+            part = dot_nt(at(u[1])[child, columns].reshape(NH, S[1]), at(table[0])[child])
+            at(f0)[...] = at(B[0])[...].astype(jnp.float32) + part
+            take(at(ur1).at[1], 2 * NQ * S[1])
+        with phase(49):
+            part = dot_nt(at(u[1])[1 - child, columns].reshape(NH, S[1]), at(table[0])[1 - child])
+            right = (at(f0)[...] + part).astype(bf)
         with phase(43):
             arrived(at(Zm[0]), at(Zmr[0]))
         with phase(44):
@@ -841,6 +871,25 @@
             with phase(45):
                 settle_all(0, 1)
                 forward(0, 1)
+        def wait_mate(l):
+            @pl.when(middle)
+            def _():
+                arrived(at(yb[l]).at[1], at(yr[l]))
+
+            @pl.when(border)
+            def _():
+                arrived(at(yb[l]), at(yr[l]))
+            if l < 3:
+                arrived(at(Zm[l]), at(Zmr[l]))
+                arrived(at(Cm[l]), at(Cmr[l]))
+
+        with phase(50):
+            arrived(at(Zm[3]), at(Zmr[3]))
+            arrived(at(Cm[3]), at(Cmr[3]))
+            for mate in range(2):
+                leaf = core if mate == 0 else 1 - core
+                block = at((C, Cm)[mate][3])[...]
+                at(folded3)[mate] = dot_nn(at(table[2])[leaf], block).astype(bf)
 
         @pl.when(border)
         def _():
@@ -856,7 +905,13 @@
             value = value.astype(bf)
             at(x0)[...] = value
 
+        farthest = jnp.where(border, across, beyond)
+        second = jnp.where(border, beyond, across)
+
         def leave(l, piece, dst, c_to):
+            for r in (farthest, second, pair):
+                push(piece(r), dst, at(Os[l]), at(Or[l]), r, c_to)
+
             @pl.when(c_to == c)
             def _():
                 pltpu.make_async_copy(piece(z), dst, at(Or[l])).start()
@@ -864,9 +919,6 @@
             @pl.when(c_to != c)
             def _():
                 push(piece(z), dst, at(Os[l]), at(Or[l]), z, c_to)
-            for d in (2, 1, 3):
-                r = (z + d) % R
-                push(piece(r), dst, at(Os[l]), at(Or[l]), r, c_to)
 
         top_here, one_here = chip == z, q // 2 == z // 2
         one_to, two_to = 2 * chip + z % 2, 2 * chip + z // 2
@@ -887,17 +939,6 @@
 
         def residual(l, index, coupled, low):
             return (at(yb[l])[index].astype(jnp.float32) - dot_nn(low, at(coupled[l])[...])).astype(bf)
-
-        def wait_mate(l):
-            @pl.when(middle)
-            def _():
-                arrived(at(yb[l]).at[1], at(yr[l]))
-
-            @pl.when(border)
-            def _():
-                arrived(at(yb[l]), at(yr[l]))
-            arrived(at(Zm[l]), at(Zmr[l]))
-            arrived(at(Cm[l]), at(Cmr[l]))
 
         with phase(52):
             wait_mate(1)
@@ -907,6 +948,11 @@
             at(xp1)[...] = value.astype(bf)
             counted(at(xp1), at(xr1), plane, at(xr1r), z, flipped(c, 2))
         side = chip % 2
+        @pl.when(border)
+        def _():
+            with phase(56):
+                settle_all(1, 2)
+                forward(1, 2)
         with phase(54):
             early = dot_nn(low, at(table[1])[side, S[1]:, :])
             arrived(at(xr1), at(xr1r))
@@ -915,8 +961,7 @@
             at(v[2])[...] = (dot_nn(value, at(table[1])[side, :S[1], :]) + early).astype(bf)
             at(x1)[...] = value
             low = at(v[2])[...]
-        with phase(56):
-            wait_mate(2)
+        wait_mate(2)
         with phase(57):
             value = dot_nn(residual(2, 0, C, low), at(Z[2])[...])
             value = value + dot_nn(residual(2, 1, Cm, low), at(Zm[2])[...])
@@ -937,24 +982,22 @@
             wait_mate(3)
         with phase(60):
             for mate in range(2):
-                leaf = core if mate == 0 else 1 - core
-                below = dot_nn(high, at(table[2])[leaf, :S[2], :])
-                below = (below + dot_nn(low, at(table[2])[leaf, S[2]:, :])).astype(bf)
-                left, right = ((C, Z), (Cm, Zm))[mate]
-                value = dot_nt(residual(3, mate, left, below), at(right[3])[...]).astype(bf)
+                below = dot_nn(high, at(folded3)[mate, :S[2], :])
+                below = below + dot_nn(low, at(folded3)[mate, S[2]:, :])
+                below = (at(yb[3])[mate].astype(jnp.float32) - below).astype(bf)
+                value = dot_nt(below, at((Z, Zm)[mate][3])[...]).astype(bf)
                 for r in range(R):
-                    at(f3)[mate * R + r] = value[:, r * K[3]:(r + 1) * K[3]]
-                leave(
-                    3, lambda r: at(f3).at[mate * R + r], placed(3, z * N + core * NH),
-                    c if mate == 0 else flipped(c, 1),
-                )
+                    piece = value[:, r * K[3]:(r + 1) * K[3]]
+                    at(f3)[mate * R + r] = jnp.concatenate([piece[:NH // 2], piece[NH // 2:]], axis=1)
+            low_row = pl.multiple_of((z * N + core * NH) // 2, 16)
+            leaf_out = outs[3].at[pl.ds(low_row, NH // 2)]
+            for mate in range(2):
+                leave(3, lambda r: at(f3).at[mate * R + r], leaf_out, c if mate == 0 else flipped(c, 1))
         with phase(61):
             for l in levels:
                 drain(0, l)
-                arrived(at(Zm[l]), at(Zms[l]))
                 if l:
                     drain(1, l)
-                    arrived(at(Cm[l]), at(Cms[l]))
                 drain_rhs(l)
                 if l < 3:
                     drain_spread(l)
@@ -965,6 +1008,11 @@
                     arrived(at(y[l]).at[pl.ds(0, 3)], at(ys[l]))
                 take(at(inner), sent[inner])
             take(at(plane), sent[plane])
+            joined = [shape for shape in z_shape + c_shape[1:] if shape[1] % 128 == 0]
+            take(at(mates), sum(elements(shape) for shape in joined))
+            for shape, copy in zip(c_shape[1:], Cm[1:]):
+                if shape[1] % 128:
+                    arrived(at(copy), at(mates1))
 
             @pl.when(jnp.logical_not(kept_here))
             def _():
@@ -1003,10 +1051,17 @@
         pltpu.make_async_copy(refs[i], refs[8 + i], arriving.at[i]).start()
     for i, (turn, source, target) in enumerate(zip(turned, refs[8:12], refs[4:8])):
         pltpu.make_async_copy(refs[i], source, arriving.at[i]).wait()
-        if turn:
-            target[...] = dot_nt(eye(target.shape[0]), source[...]).astype(target.dtype)
+        rows, lanes = source.shape
+        if not turn:
+            target[...] = source[...]
+        elif target.shape == (lanes, rows):
+            target[...] = dot_nt(eye(lanes), source[...]).astype(target.dtype)
         else:
-            target[...] = source[...]
+            both = dot_nt(eye(lanes), source[...]).astype(target.dtype)
+            pieces = []
+            for low in range(0, rows, 16):
+                pieces += [both[:lanes // 2, low:low + 16], both[lanes // 2:, low:low + 16]]
+            target[...] = jnp.concatenate(pieces, axis=1)
 
 
 def fused_device(*blocks):
@@ -1028,8 +1083,7 @@
     solved = pl.pallas_call(
         kernel,
         out_shape=tuple(
-            jax.ShapeDtypeStruct((width, strip), blocks[0].dtype)
-            for width, strip in zip(plan.width, plan.strip)
+            jax.ShapeDtypeStruct(shape, blocks[0].dtype) for shape in plan.result_shapes()
         ),
         in_specs=[anywhere] * 14,
         out_specs=(pl.BlockSpec(memory_space=pl.ANY),) * 4,
@@ -1042,8 +1096,8 @@
     solved = pl.pallas_call(
         functools.partial(hand_on, turned),
         out_shape=tuple(
-            jax.ShapeDtypeStruct(block.shape[::-1] if turn else block.shape, block.dtype)
-            for block, turn in zip(solved, turned)
+            jax.ShapeDtypeStruct((strip, width) if turn else (width, strip), blocks[0].dtype)
+            for width, strip, turn in zip(plan.width, plan.strip, turned)
         ),
         in_specs=[pl.BlockSpec(memory_space=pl.ANY)] * 4,
         out_specs=(vmem,) * 4,

time: 52.9 us -> 51.1 us (0.966)
  Pallas kernels: 52.1 us -> 50.4 us
    pallas_call x1, Pallas kernels: 50.9 us -> 49.1 us  [fused_device(): pl.pallas_call(kernel, out_shape=tuple((jax.ShapeDtypeStruct(shape, block...]
where the time goes in v3:
time: 51.1 us; the launch traced here: 51 us
  Pallas kernels  50.4 us (99%)
  between operations  0.64 us (1%)
    pallas_call x1, Pallas kernels, fused_device(): pl.pallas_call(kernel, out_shape=tuple((jax.ShapeDtypeStruct(shape, block...  49.1 us
    pallas_call x1, Pallas kernels, fused_device(): pl.pallas_call(functools.partial(hand_on, turned), out_shape=tuple((jax.S...  1.25 us

profile of v3, /device:TPU:0, one launch (start us, length us, event | category | flops | bytes accessed | tf_op | source)
XLA Modules:
  0.0 51.0 jit_solution(9608374675740876233)
XLA Ops:
  0.6 49.1 %shard_map.165 = (bf16[32,256]{1,0:T(8,128)(2,1)S(1)}, bf16[64,192]{1,0:T(8,128)(2,1)S(1)}, bf16[128,128]{1,0:T(8,128)(2,1)S(1)}, bf16[128,128]{1,0:T(8,128)(2,1)S(1)}) custom-call(bf16[128,256]{1,0:T(8,128)(2,1)} %refs_0_.1, bf16[192,192]{1,0:T(8,128)(2,1)} %refs_1_.1, bf16[256,128]{1,0:T(8,128)(2,1)} %refs_2_.1, bf16[64,256]{1,0:T(8,128)(2,1)} %bitcast.5, ...), custom_call_target="tpu_custom_call" | custom-call | tf_op jit(solution)/shard_map/pallas_call | solution.py:1083
  49.8 1.2 %shard_map.166 = (bf16[32,256]{1,0:T(8,128)(2,1)}, bf16[64,192]{1,0:T(8,128)(2,1)}, bf16[128,128]{1,0:T(8,128)(2,1)}, bf16[64,256]{1,0:T(8,128)(2,1)}) custom-call(bf16[32,256]{1,0:T(8,128)(2,1)S(1)} %get-tuple-element.12.refs_0_, bf16[64,192]{1,0:T(8,128)(2,1)S(1)} %get-tuple-element.13.refs_1_, bf16[128,128]{1,0:T(8,128)(2,1)S(1)} %get-tuple-element.14.refs_2_, ...), custom_call_target="tpu_custom_call" | custom-call | tf_op jit(solution)/shard_map/pallas_call | solution.py:1096

commit v4 on v3

--- a/solution.py
+++ b/solution.py
@@ -364,6 +364,8 @@
     plane, inner, beside = sems(), sems(), sems()
     scratch.append(pltpu.SemaphoreType.REGULAR)
     ready = len(scratch) - 1
+    scratch.append(pltpu.SemaphoreType.REGULAR)
+    ready_group = len(scratch) - 1
     span = ref((plan.span_rows(), 128))
 
     def kernel(*refs):
@@ -406,7 +408,8 @@
             pltpu.make_async_copy(view, view, sem).wait()
 
         barrier = pltpu.get_barrier_semaphore()
-        mates_here = [(z, flipped(c, m)) for m in range(1, CC)]
+        group_here = [(z, flipped(c, m)) for m in range(1, G[1])]
+        opposite = (z, flipped(c, G[1]))
 
         def greet(semaphore, *friends):
             for friend in friends:
@@ -416,7 +419,11 @@
 
         @pl.when(middle)
         def _():
-            greet(barrier, (across, c), (beyond, c), *mates_here)
+            greet(barrier, (across, c), (beyond, c), *group_here)
+
+        @pl.when(border)
+        def _():
+            greet(barrier, opposite)
 
         raws = [(rhs[1], at(rhs_raw))]
         for l in levels:
@@ -640,11 +647,11 @@
         with phase(2):
             @pl.when(middle)
             def _():
-                pl.semaphore_wait(barrier, CC + 1)
+                pl.semaphore_wait(barrier, G[1] + 1)
 
             @pl.when(border)
             def _():
-                pl.semaphore_wait(barrier, 2)
+                pl.semaphore_wait(barrier, 3)
 
         with phase(3):
             own_send(0, 3)
@@ -676,7 +683,18 @@
                 for l in (3, 2, 1):
                     own_out(0, l)
                     own_out(1, l)
-                greet(at(ready), *mates_here)
+
+            @pl.when(border)
+            def _():
+                greet(at(ready), opposite)
+                pl.semaphore_wait(at(ready), 1)
+                greet(at(ready), (pair, c))
+
+        def last_send(turn):
+            @pl.when(turn)
+            def _():
+                own_send(0, 0)
+
         make_table(2)
 
         @pl.when(middle)
@@ -686,9 +704,9 @@
                 right = dot_nt(eye(N2), at(B[3])[...]).astype(bf)
                 settle_all(0, 3)
                 start_rhs(0)
-                own_send(0, 0)
-                pl.semaphore_wait(at(ready), CC - 1)
-                greet(at(ready), (pair, c))
+                last_send(core == 0)
+                pl.semaphore_wait(at(ready), 1)
+                greet(at(ready_group), *group_here)
             with phase(32):
                 solved = dot_nn(right, at(Z[3])[...]).astype(bf)
                 at(y[3])[...] = solved.reshape(4, NH, L[3])
@@ -697,6 +715,8 @@
                 at(u[3])[core] = (-dot_nt(solved, at(C[3])[...])).astype(bf)
                 here = at(u[3]).at[core]
                 counted(here, here, inner, at(ur[3]), z, flipped(c, 1))
+                pl.semaphore_wait(at(ready_group), G[1] - 1)
+                greet(at(ready), (pair, c))
                 pass_on(0, 3)
                 pass_on(1, 3)
         spread_rhs(2)
@@ -733,7 +753,7 @@
                 child = (c // G[2]) % 2
                 at(u[2])[child, core] = own.astype(bf).reshape(G[1], NQ, S[2])
                 here = at(u[2]).at[child, core]
-                for m in range(1, G[1]):
+                for m in (3, 2, 1):
                     counted(here, here, inner, at(ur[2]), z, flipped(c, m))
         make_table(0)
         q, child = c % G[1], (c // G[1]) % 2
@@ -767,12 +787,13 @@
             with phase(17):
                 coupled = dot_nt(solved, at(C[1])[...])
                 at(up1)[...] = coupled.astype(bf).reshape(2, G[1], NQ, S[1])
-                for m in range(1, G[1]):
+                for m in (3, 2, 1):
                     src = at(up1).at[1 - half, flipped(q, m)]
                     counted(src, at(ut1).at[m], inner, at(ut1r), pair, flipped(c, m))
-                for m in range(1, G[1]):
+                for m in (3, 2, 1):
                     src = at(up1).at[half, flipped(q, m)]
                     counted(src, at(ut1).at[m], inner, at(ut1r), z, flipped(c, m))
+                last_send(core == 1)
                 pair_of = [at(u[2])[i, :, q].reshape(2 * NQ, S[2]) for i in range(2)]
                 kept = gathered(1, S[1], S[1], *pair_of)
                 at(h1)[...] = kept.astype(bf).reshape(2, NQ, S[1])
@@ -798,7 +819,8 @@
                     settle_all(kind, l)
                     if (kind, l) == (0, 3):
                         start_rhs(0)
-                        own_send(0, 0)
+                    if (kind, l) != (1, 3):
+                        last_send(core == (0 if l == 3 else 1))
                     forward(kind, l)
                 spread_rhs(0)
                 arrived(at(ut1), at(ut1r))
@@ -817,7 +839,7 @@
                 at(u[1])[child, q] = (at(h1)[half].astype(jnp.float32) - value).astype(bf)
         here = at(u[1]).at[child, q]
         kept_here = q // 2 == core
-        for m in range(2, CC, 2):
+        for m in (6, 4, 2):
             rsem = at(ur1).at[0 if m == 2 else 1]
             counted(here, here, plane, rsem, z, flipped(2 * chip + q // 2, m))
 
@@ -908,17 +930,19 @@
         farthest = jnp.where(border, across, beyond)
         second = jnp.where(border, beyond, across)
 
-        def leave(l, piece, dst, c_to):
+        def leave(l, piece, dst, c_to, kept=None):
             for r in (farthest, second, pair):
                 push(piece(r), dst, at(Os[l]), at(Or[l]), r, c_to)
 
-            @pl.when(c_to == c)
-            def _():
-                pltpu.make_async_copy(piece(z), dst, at(Or[l])).start()
-
-            @pl.when(c_to != c)
-            def _():
-                push(piece(z), dst, at(Os[l]), at(Or[l]), z, c_to)
+            keep = lambda: pltpu.make_async_copy(piece(z), dst, at(Or[l])).start()
+            give = lambda: push(piece(z), dst, at(Os[l]), at(Or[l]), z, c_to)
+            if kept is None:
+                pl.when(c_to == c)(keep)
+                pl.when(c_to != c)(give)
+            elif kept:
+                keep()
+            else:
+                give()
 
         top_here, one_here = chip == z, q // 2 == z // 2
         one_to, two_to = 2 * chip + z % 2, 2 * chip + z // 2
@@ -928,7 +952,7 @@
 
         @pl.when(top_here)
         def _():
-            leave(0, top_piece, outs[0], c)
+            leave(0, top_piece, outs[0], c, True)
 
         def placed(l, low):
             return outs[l].at[pl.ds(pl.multiple_of(low, 16), NH)]
@@ -992,7 +1016,7 @@
             low_row = pl.multiple_of((z * N + core * NH) // 2, 16)
             leaf_out = outs[3].at[pl.ds(low_row, NH // 2)]
             for mate in range(2):
-                leave(3, lambda r: at(f3).at[mate * R + r], leaf_out, c if mate == 0 else flipped(c, 1))
+                leave(3, lambda r: at(f3).at[mate * R + r], leaf_out, flipped(c, mate), mate == 0)
         with phase(61):
             for l in levels:
                 drain(0, l)
@@ -1046,22 +1070,29 @@
 
 
 def hand_on(turned, *refs):
-    arriving = refs[12]
-    for i in range(4):
-        pltpu.make_async_copy(refs[i], refs[8 + i], arriving.at[i]).start()
-    for i, (turn, source, target) in enumerate(zip(turned, refs[8:12], refs[4:8])):
-        pltpu.make_async_copy(refs[i], source, arriving.at[i]).wait()
-        rows, lanes = source.shape
-        if not turn:
-            target[...] = source[...]
-        elif target.shape == (lanes, rows):
-            target[...] = dot_nt(eye(lanes), source[...]).astype(target.dtype)
+    given, results, staged, made = refs[:4], refs[4:8], refs[8:12], refs[12:16]
+    arriving, leaving = refs[16], refs[17]
+    copies = []
+    for i in (3, 2, 1, 0):
+        if turned[i]:
+            pltpu.make_async_copy(given[i], staged[i], arriving.at[i]).start()
         else:
-            both = dot_nt(eye(lanes), source[...]).astype(target.dtype)
+            copies.append(pltpu.make_async_copy(given[i], results[i], leaving.at[i]))
+            copies[-1].start()
+    for i in (3, 2):
+        pltpu.make_async_copy(given[i], staged[i], arriving.at[i]).wait()
+        rows, lanes = staged[i].shape
+        both = dot_nt(eye(lanes), staged[i][...]).astype(made[i].dtype)
+        if made[i].shape != (lanes, rows):
             pieces = []
             for low in range(0, rows, 16):
                 pieces += [both[:lanes // 2, low:low + 16], both[lanes // 2:, low:low + 16]]
-            target[...] = jnp.concatenate(pieces, axis=1)
+            both = jnp.concatenate(pieces, axis=1)
+        made[i][...] = both
+        copies.append(pltpu.make_async_copy(made[i], results[i], leaving.at[i]))
+        copies[-1].start()
+    for copy in copies:
+        copy.wait()
 
 
 def fused_device(*blocks):
@@ -1078,7 +1109,6 @@
         if narrow(blocks[at].shape[1]):
             blocks[at] = blocks[at].T
     blocks = [pltpu.with_memory_space_constraint(block, pltpu.HBM) for block in blocks]
-    vmem = pl.BlockSpec(memory_space=pltpu.VMEM)
     anywhere = pl.BlockSpec(memory_space=pltpu.HBM)
     solved = pl.pallas_call(
         kernel,
@@ -1093,16 +1123,18 @@
         ),
     )(*blocks)
     turned = [not narrow(width) for width in plan.width]
+    final = [
+        (strip, width) if turn else (width, strip)
+        for width, strip, turn in zip(plan.width, plan.strip, turned)
+    ]
     solved = pl.pallas_call(
         functools.partial(hand_on, turned),
-        out_shape=tuple(
-            jax.ShapeDtypeStruct((strip, width) if turn else (width, strip), blocks[0].dtype)
-            for width, strip, turn in zip(plan.width, plan.strip, turned)
-        ),
+        out_shape=tuple(jax.ShapeDtypeStruct(shape, blocks[0].dtype) for shape in final),
         in_specs=[pl.BlockSpec(memory_space=pl.ANY)] * 4,
-        out_specs=(vmem,) * 4,
+        out_specs=(pl.BlockSpec(memory_space=pltpu.HBM),) * 4,
         scratch_shapes=[pltpu.VMEM(block.shape, block.dtype) for block in solved]
-        + [pltpu.SemaphoreType.DMA((4,))],
+        + [pltpu.VMEM(shape, blocks[0].dtype) for shape in final]
+        + [pltpu.SemaphoreType.DMA((4,))] * 2,
         compiler_params=pltpu.CompilerParams(vmem_limit_bytes=2**20),
     )(*solved)
     return tuple(block if turn else block.T for block, turn in zip(solved, turned))

time: 51.1 us -> 50.9 us (level)
  no operation moved by 1% of the time
where the time goes in v4:
time: 50.9 us; the launch traced here: 50.7 us
  Pallas kernels  50.1 us (98%)
  between operations  0.64 us (1%)
    pallas_call x1, Pallas kernels, fused_device(): pl.pallas_call(kernel, out_shape=tuple((jax.ShapeDtypeStruct(shape, block...  48.9 us
    pallas_call x1, Pallas kernels, fused_device(): pl.pallas_call(functools.partial(hand_on, turned), out_shape=tuple((jax.S...  1.21 us

profile of v4, /device:TPU:0, one launch (start us, length us, event | category | flops | bytes accessed | tf_op | source)
XLA Modules:
  0.0 50.7 jit_solution(2004452774457971221)
XLA Ops:
  0.6 48.9 %shard_map.165 = (bf16[32,256]{1,0:T(8,128)(2,1)S(1)}, bf16[64,192]{1,0:T(8,128)(2,1)S(1)}, bf16[128,128]{1,0:T(8,128)(2,1)S(1)}, bf16[128,128]{1,0:T(8,128)(2,1)S(1)}) custom-call(bf16[128,256]{1,0:T(8,128)(2,1)} %refs_0_.1, bf16[192,192]{1,0:T(8,128)(2,1)} %refs_1_.1, bf16[256,128]{1,0:T(8,128)(2,1)} %refs_2_.1, bf16[64,256]{1,0:T(8,128)(2,1)} %bitcast.5, ...), custom_call_target="tpu_custom_call" | custom-call | tf_op jit(solution)/shard_map/pallas_call | solution.py:1113
  49.5 1.2 %shard_map.166 = (bf16[32,256]{1,0:T(8,128)(2,1)}, bf16[64,192]{1,0:T(8,128)(2,1)}, bf16[128,128]{1,0:T(8,128)(2,1)}, bf16[64,256]{1,0:T(8,128)(2,1)}) custom-call(bf16[32,256]{1,0:T(8,128)(2,1)S(1)} %get-tuple-element.12.refs_0_, bf16[64,192]{1,0:T(8,128)(2,1)S(1)} %get-tuple-element.13.refs_1_, bf16[128,128]{1,0:T(8,128)(2,1)S(1)} %get-tuple-element.14.refs_2_, ...), custom_call_target="tpu_custom_call" | custom-call | tf_op jit(solution)/shard_map/pallas_call | solution.py:1130

commit v5 on v4

--- a/solution.py
+++ b/solution.py
@@ -359,7 +359,7 @@
     v = [None] + [ref((NH, S[l])) for l in (1, 2)]
     x1, x2 = ref((NH, S[1])), ref((NH, S[2]))
     f1, f3 = ref((R, NH, K[1])), ref((2 * R, NH // 2, 2 * K[3]))
-    folded3 = ref((2, 2 * S[2], L[3]))
+    folded3, folded1 = ref((2, 2 * S[2], L[3])), ref((2, S[0], L[1]))
     Os, Or = [sems() for _ in levels], [sems() for _ in levels]
     plane, inner, beside = sems(), sems(), sems()
     scratch.append(pltpu.SemaphoreType.REGULAR)
@@ -785,11 +785,16 @@
             with phase(16):
                 settle_all(1, 1)
             with phase(17):
-                coupled = dot_nt(solved, at(C[1])[...])
-                at(up1)[...] = coupled.astype(bf).reshape(2, G[1], NQ, S[1])
+                def couple(part):
+                    rows = at(y[1])[pl.ds(pl.multiple_of(2 * part, 2), 2)].reshape(N, L[1])
+                    value = dot_nt(rows, at(C[1])[...]).astype(bf)
+                    at(up1)[part] = value.reshape(G[1], NQ, S[1])
+
+                couple(1 - half)
                 for m in (3, 2, 1):
                     src = at(up1).at[1 - half, flipped(q, m)]
                     counted(src, at(ut1).at[m], inner, at(ut1r), pair, flipped(c, m))
+                couple(half)
                 for m in (3, 2, 1):
                     src = at(up1).at[half, flipped(q, m)]
                     counted(src, at(ut1).at[m], inner, at(ut1r), z, flipped(c, m))
@@ -903,6 +908,7 @@
                 arrived(at(yb[l]), at(yr[l]))
             if l < 3:
                 arrived(at(Zm[l]), at(Zmr[l]))
+            if l == 2:
                 arrived(at(Cm[l]), at(Cmr[l]))
 
         with phase(50):
@@ -918,6 +924,12 @@
             with phase(48):
                 settle_all(1, 1)
                 forward(1, 1)
+        with phase(57):
+            at(folded1)[0] = dot_nn(at(table[0])[child], at(C[1])[...]).astype(bf)
+        with phase(52):
+            arrived(at(Cm[1]), at(Cmr[1]))
+        with phase(58):
+            at(folded1)[1] = dot_nn(at(table[0])[child], at(Cm[1])[...]).astype(bf)
         with phase(46):
             arrived(at(xr0).at[pl.ds(1, chips - 1)], at(xr0r))
         with phase(47):
@@ -957,26 +969,27 @@
         def placed(l, low):
             return outs[l].at[pl.ds(pl.multiple_of(low, 16), NH)]
 
-        with phase(51):
-            at(v[1])[...] = dot_nn(value, at(table[0])[child]).astype(bf)
-            low = at(v[1])[...]
-
         def residual(l, index, coupled, low):
             return (at(yb[l])[index].astype(jnp.float32) - dot_nn(low, at(coupled[l])[...])).astype(bf)
 
-        with phase(52):
-            wait_mate(1)
+        wait_mate(1)
         with phase(53):
-            value = dot_nn(residual(1, 0, C, low), at(Z[1])[...])
-            value = value + dot_nn(residual(1, 1, Cm, low), at(Zm[1])[...])
-            at(xp1)[...] = value.astype(bf)
+            total = 0.0
+            for mate in range(2):
+                below = at(yb[1])[mate].astype(jnp.float32) - dot_nn(value, at(folded1)[mate])
+                total = total + dot_nn(below.astype(bf), at((Z, Zm)[mate][1])[...])
+            at(xp1)[...] = total.astype(bf)
             counted(at(xp1), at(xr1), plane, at(xr1r), z, flipped(c, 2))
+            top = value
         side = chip % 2
         @pl.when(border)
         def _():
             with phase(56):
                 settle_all(1, 2)
                 forward(1, 2)
+        with phase(51):
+            at(v[1])[...] = dot_nn(top, at(table[0])[child]).astype(bf)
+            low = at(v[1])[...]
         with phase(54):
             early = dot_nn(low, at(table[1])[side, S[1]:, :])
             arrived(at(xr1), at(xr1r))

time: 50.9 us -> 50.5 us (level)
  no operation moved by 1% of the time
where the time goes in v5:
time: 50.5 us; the launch traced here: 50.4 us
  Pallas kernels  49.7 us (98%)
  between operations  0.64 us (1%)
    pallas_call x1, Pallas kernels, fused_device(): pl.pallas_call(kernel, out_shape=tuple((jax.ShapeDtypeStruct(shape, block...  48.5 us
    pallas_call x1, Pallas kernels, fused_device(): pl.pallas_call(functools.partial(hand_on, turned), out_shape=tuple((jax.S...  1.21 us

profile of v5, /device:TPU:0, one launch (start us, length us, event | category | flops | bytes accessed | tf_op | source)
XLA Modules:
  0.0 50.4 jit_solution(12968263769727944962)
XLA Ops:
  0.6 48.5 %shard_map.165 = (bf16[32,256]{1,0:T(8,128)(2,1)S(1)}, bf16[64,192]{1,0:T(8,128)(2,1)S(1)}, bf16[128,128]{1,0:T(8,128)(2,1)S(1)}, bf16[128,128]{1,0:T(8,128)(2,1)S(1)}) custom-call(bf16[128,256]{1,0:T(8,128)(2,1)} %refs_0_.1, bf16[192,192]{1,0:T(8,128)(2,1)} %refs_1_.1, bf16[256,128]{1,0:T(8,128)(2,1)} %refs_2_.1, bf16[64,256]{1,0:T(8,128)(2,1)} %bitcast.5, ...), custom_call_target="tpu_custom_call" | custom-call | tf_op jit(solution)/shard_map/pallas_call | solution.py:1126
  49.2 1.2 %shard_map.166 = (bf16[32,256]{1,0:T(8,128)(2,1)}, bf16[64,192]{1,0:T(8,128)(2,1)}, bf16[128,128]{1,0:T(8,128)(2,1)}, bf16[64,256]{1,0:T(8,128)(2,1)}) custom-call(bf16[32,256]{1,0:T(8,128)(2,1)S(1)} %get-tuple-element.12.refs_0_, bf16[64,192]{1,0:T(8,128)(2,1)S(1)} %get-tuple-element.13.refs_1_, bf16[128,128]{1,0:T(8,128)(2,1)S(1)} %get-tuple-element.14.refs_2_, ...), custom_call_target="tpu_custom_call" | custom-call | tf_op jit(solution)/shard_map/pallas_call | solution.py:1143

commit v6 on v5

--- a/solution.py
+++ b/solution.py
@@ -769,6 +769,7 @@
             with phase(14):
                 settle_all(0, 1)
                 pass_on(0, 1)
+                last_send(core == 1)
             with phase(10):
                 at(early1)[...] = dot_nt(at(B1)[...], at(Z[1])[...])
                 for i in range(2):
@@ -798,7 +799,6 @@
                 for m in (3, 2, 1):
                     src = at(up1).at[half, flipped(q, m)]
                     counted(src, at(ut1).at[m], inner, at(ut1r), z, flipped(c, m))
-                last_send(core == 1)
                 pair_of = [at(u[2])[i, :, q].reshape(2 * NQ, S[2]) for i in range(2)]
                 kept = gathered(1, S[1], S[1], *pair_of)
                 at(h1)[...] = kept.astype(bf).reshape(2, NQ, S[1])
@@ -962,10 +962,6 @@
         def top_piece(r):
             return at(x0).at[:, pl.ds(pl.multiple_of(r * K[0], 128), K[0])]
 
-        @pl.when(top_here)
-        def _():
-            leave(0, top_piece, outs[0], c, True)
-
         def placed(l, low):
             return outs[l].at[pl.ds(pl.multiple_of(low, 16), NH)]
 
@@ -981,6 +977,11 @@
             at(xp1)[...] = total.astype(bf)
             counted(at(xp1), at(xr1), plane, at(xr1r), z, flipped(c, 2))
             top = value
+
+        @pl.when(top_here)
+        def _():
+            leave(0, top_piece, outs[0], c, True)
+
         side = chip % 2
         @pl.when(border)
         def _():

time: 50.5 us -> 50.3 us (level)
  no operation moved by 1% of the time
where the time goes in v6:
time: 50.3 us; the launch traced here: 50.2 us
  Pallas kernels  49.5 us (98%)
  between operations  0.64 us (1%)
    pallas_call x1, Pallas kernels, fused_device(): pl.pallas_call(kernel, out_shape=tuple((jax.ShapeDtypeStruct(shape, block...  48.3 us
    pallas_call x1, Pallas kernels, fused_device(): pl.pallas_call(functools.partial(hand_on, turned), out_shape=tuple((jax.S...  1.21 us

profile of v6, /device:TPU:0, one launch (start us, length us, event | category | flops | bytes accessed | tf_op | source)
XLA Modules:
  0.0 50.2 jit_solution(13274817417298891919)
XLA Ops:
  0.6 48.3 %shard_map.165 = (bf16[32,256]{1,0:T(8,128)(2,1)S(1)}, bf16[64,192]{1,0:T(8,128)(2,1)S(1)}, bf16[128,128]{1,0:T(8,128)(2,1)S(1)}, bf16[128,128]{1,0:T(8,128)(2,1)S(1)}) custom-call(bf16[128,256]{1,0:T(8,128)(2,1)} %refs_0_.1, bf16[192,192]{1,0:T(8,128)(2,1)} %refs_1_.1, bf16[256,128]{1,0:T(8,128)(2,1)} %refs_2_.1, bf16[64,256]{1,0:T(8,128)(2,1)} %bitcast.5, ...), custom_call_target="tpu_custom_call" | custom-call | tf_op jit(solution)/shard_map/pallas_call | solution.py:1127
  48.9 1.2 %shard_map.166 = (bf16[32,256]{1,0:T(8,128)(2,1)}, bf16[64,192]{1,0:T(8,128)(2,1)}, bf16[128,128]{1,0:T(8,128)(2,1)}, bf16[64,256]{1,0:T(8,128)(2,1)}) custom-call(bf16[32,256]{1,0:T(8,128)(2,1)S(1)} %get-tuple-element.12.refs_0_, bf16[64,192]{1,0:T(8,128)(2,1)S(1)} %get-tuple-element.13.refs_1_, bf16[128,128]{1,0:T(8,128)(2,1)S(1)} %get-tuple-element.14.refs_2_, ...), custom_call_target="tpu_custom_call" | custom-call | tf_op jit(solution)/shard_map/pallas_call | solution.py:1144
